TPU v7x, 128 devices: a whole 4x4x4 slice. The times are simulated.
128 devices in a mesh: group: 4 (over x), dev: 32 (over y, z, core).
Axes of the slice: x: 4, y: 4, z: 4, core: 2. Of those that a mesh axis runs over, the one named last changes fastest.
Arguments:
- node_feats: bfloat16 [32768, 1024], P(('group', 'dev')), may hold values from -60 to 60
- w_gcn: bfloat16 [1024, 1024], replicated, may hold values from -0.1875 to 0.1875
- adj_tiles: bfloat16 [256, 16, 128, 128], P(('group', 'dev')), may hold values from -0.125 to 0.125
- neighbor_blocks: int32 [256, 16], P(('group', 'dev')), may hold values from 0 to 21, all different within a row
- inner_rows: int32 [128, 32, 64], P(('group', 'dev')), may hold values from 0 to 255
- outer_rows: int32 [128, 4, 128], P(('group', 'dev')), may hold values from 0 to 255
- w_qkv: bfloat16 [1024, 3072], replicated, may hold values from -0.1875 to 0.1875
- key_blocks: int32 [256, 16], P('group'), may hold values from 0 to 63, all different within a row
- key_counts: int32 [256], P('group'), may hold values from 1 to 16
- w_out: bfloat16 [1024, 1024], replicated, may hold values from -0.1875 to 0.1875
- w_up: bfloat16 [1024, 2048], replicated, may hold values from -0.1875 to 0.1875
- w_down: bfloat16 [2048, 1024], replicated, may hold values from -0.125 to 0.125
Outputs:
- layer_out: bfloat16 [32768, 1024], P(('group', 'dev'))
Inputs may be any that keep to these rules, and one draw needn't show every extreme that they name: `inner_rows`: row numbers of the sending device. `outer_rows`: row numbers of the sending device. `neighbor_blocks`: table block numbers; the 16 entries of a row differ. `key_blocks`: the 16 entries of a row differ.
All inputs are finite; a program needn't handle non-finite values.
Results may differ from a plain program's by a relative error of at most 0.012.
The roundings to bfloat16 on the way count: a program that leaves them out, or rounds other values in their place, can miss the bound.
Values may be sent and summed in bfloat16 or wider, within the bound.
A program may use at most 128 MiB of HBM per device.

v0:
```python
import jax
import jax.numpy as jnp
from jax import lax
from jax.sharding import PartitionSpec as P

H = 32


def layer_norm(values):
    average = jnp.mean(values, axis=-1, keepdims=True)
    centered = values - average
    variance = jnp.mean(centered * centered, axis=-1, keepdims=True)
    return centered / jnp.sqrt(variance + 1e-05)


def per_device(
    node_feats,
    w_gcn,
    adj_tiles,
    neighbor_blocks,
    inner_rows,
    outer_rows,
    w_qkv,
    key_blocks,
    key_counts,
    w_out,
    w_up,
    w_down,
):
    row_count = node_feats.shape[0]
    width = node_feats.shape[1]
    block_rows = adj_tiles.shape[-1]
    peers = lax.axis_size("dev")
    clusters = lax.axis_size("group")
    head_size = width // H
    local_heads = H // peers
    head_cols = local_heads * head_size
    gcn_rows = jnp.dot(node_feats, w_gcn, preferred_element_type=jnp.float32).astype(jnp.bfloat16)
    qkv_split = jnp.einsum(
        "rd,dtph->pthr",
        node_feats,
        w_qkv.reshape(width, 3, peers, head_cols),
        preferred_element_type=jnp.float32,
    ).astype(jnp.bfloat16)
    send_inner = gcn_rows[inner_rows[0].reshape(-1)].reshape(peers, -1, width)
    inner_part = lax.all_to_all(send_inner, "dev", split_axis=0, concat_axis=0, tiled=True).reshape(
        -1, width
    )
    send_outer = gcn_rows[outer_rows[0].reshape(-1)].reshape(clusters, -1, width)
    outer_part = lax.all_to_all(
        send_outer, "group", split_axis=0, concat_axis=0, tiled=True
    ).reshape(-1, width)
    head_parts = lax.all_to_all(qkv_split, "dev", split_axis=0, concat_axis=3, tiled=True)
    table = jnp.concatenate([gcn_rows, inner_part, outer_part], axis=0)
    table_count = table.shape[0] // block_rows
    selector = (
        neighbor_blocks[:, :, None] == jnp.arange(table_count, dtype=jnp.int32)[None, None, :]
    ).astype(jnp.bfloat16)
    spread = jnp.einsum(
        "bst,bsij->bitj", selector, adj_tiles, preferred_element_type=jnp.float32
    ).astype(jnp.bfloat16)
    agg = jnp.dot(
        spread.reshape(row_count, table_count * block_rows),
        table,
        preferred_element_type=jnp.float32,
    )
    features = node_feats.astype(jnp.float32)
    local_branch = layer_norm(features + agg)
    group_rows = row_count * peers
    block_total = group_rows // block_rows
    per_step = 8
    steps_total = block_total // per_step
    head_parts = head_parts.reshape(3, local_heads, head_size, block_total, block_rows)
    query_part = (
        head_parts[0]
        .reshape(local_heads, head_size, steps_total, per_step, block_rows)
        .transpose(2, 0, 1, 3, 4)
    )
    key_value = head_parts[1:3]
    scale = 1.0 / head_size**0.5
    slot_count = key_blocks.shape[1]

    def attend(inputs):
        picks, counts, queries = inputs
        picker = (
            picks[:, :, None] == jnp.arange(block_total, dtype=jnp.int32)[None, None, :]
        ).astype(jnp.bfloat16)
        picked = jnp.einsum(
            "qst,kletj->kleqsj", picker, key_value, preferred_element_type=jnp.float32
        ).astype(jnp.bfloat16)
        keys_here = picked[0]
        values_here = picked[1]
        scores = (
            jnp.einsum("leqi,leqsj->qlisj", queries, keys_here, preferred_element_type=jnp.float32)
            * scale
        )
        live = jnp.arange(slot_count, dtype=jnp.int32)[None, :] < counts[:, None]
        scores = jnp.where(live[:, None, None, :, None], scores, -jnp.inf)
        highest = jnp.max(scores, axis=(3, 4), keepdims=True)
        expos = jnp.exp(scores - highest)
        totals = jnp.sum(expos, axis=(3, 4), keepdims=True)
        probs = (expos / totals).astype(jnp.bfloat16)
        mixed = jnp.einsum(
            "qlisj,leqsj->leqi", probs, values_here, preferred_element_type=jnp.float32
        )
        return mixed.astype(jnp.bfloat16)

    attended = lax.map(
        attend,
        (
            key_blocks.reshape(steps_total, per_step, slot_count),
            key_counts.reshape(steps_total, per_step),
            query_part,
        ),
    )
    attended = attended.transpose(1, 2, 0, 3, 4).reshape(head_cols, group_rows)
    returned = lax.all_to_all(attended, "dev", split_axis=1, concat_axis=0, tiled=True)
    projected = lax.dot_general(
        returned, w_out, (((0,), (0,)), ((), ())), preferred_element_type=jnp.float32
    )
    attn_branch = layer_norm(features + projected)
    summed = local_branch + attn_branch
    summed_in = summed.astype(jnp.bfloat16)
    activated = jax.nn.gelu(jnp.dot(summed_in, w_up, preferred_element_type=jnp.float32)).astype(
        jnp.bfloat16
    )
    layer_out = layer_norm(summed + jnp.dot(activated, w_down, preferred_element_type=jnp.float32))
    return layer_out.astype(jnp.bfloat16)


def solution(mesh):
    placed = (
        P(("group", "dev"), None),
        P(),
        P(("group", "dev"), None, None, None),
        P(("group", "dev"), None),
        P(("group", "dev"), None, None),
        P(("group", "dev"), None, None),
        P(),
        P("group", None),
        P("group"),
        P(),
        P(),
        P(),
    )
    return jax.shard_map(
        per_device, mesh=mesh, in_specs=placed, out_specs=P(("group", "dev"), None), check_vma=False
    )
```

profile of v0, /device:TPU:1, one launch (start us, length us, event | category | flops | bytes accessed | tf_op | source)
XLA Modules:
  0.0 230.8 jit_solution(15922654847049729855)
XLA Ops:
  0.0 8.8 %copy.37 = bf16[1024,3072]{0,1:T(8,128)(2,1)} copy(bf16[1024,3072]{1,0:T(8,128)(2,1)} %param.20) | data formatting | bytes 12582912 | tf_op args[6]
  8.8 4.6 %fusion.31 = bf16[32,3,32,256]{3,2,0,1:T(8,128)(2,1)S(1)} fusion(bf16[1024,3,32,32]{0,3,2,1:T(8,128)(2,1)} %bitcast.121, bf16[256,1024]{1,0:T(8,128)(2,1)S(1)} %copy-done.3), kind=kOutput, calls=%fused_computation.47 | convolution fusion | flops 1611399168 | bytes 8388608 | tf_op jit(solution)/shard_map/rd,dtph->pthr/dot_general | solution.py:39
  14.8 9.7 %all-to-all-start.2 = ((bf16[32,3,32,256]{3,2,1,0:T(8,128)(2,1)}), bf16[32,3,32,256]{3,2,1,0:T(8,128)(2,1)}, u32[]{:S(2)}, u32[]{:S(2)}) async-start(bf16[32,3,32,256]{3,2,1,0:T(8,128)(2,1)} %copy.38), calls=%async_computation.2 | async-start | bytes 3145728 | tf_op jit(solution)/shard_map/all_to_all | solution.py:53
  24.7 2.3 convolution_convert_fusion.2
  27.0 2.8 %gather_fusion.1 = bf16[512,1024]{1,0:T(8,128)(2,1)} fusion(bf16[256,1024]{1,0:T(8,128)(2,1)S(1)} %convolution_convert_fusion.2, s32[1024]{0:T(1024)S(1)} %pad_clamp_fusion), kind=kCustom, calls=%fused_computation.1 | custom fusion | bytes 2099200 | tf_op jit(solution)/shard_map/gather | solution.py:49
  29.8 17.3 %all-to-all-done.2 = bf16[32,3,32,256]{3,2,1,0:T(8,128)(2,1)} async-done(((bf16[32,3,32,256]{3,2,1,0:T(8,128)(2,1)}), bf16[32,3,32,256]{3,2,1,0:T(8,128)(2,1)}, u32[]{:S(2)}, u32[]{:S(2)}) %all-to-all-start.2) | async-done | bytes 1572896 | tf_op jit(solution)/shard_map/all_to_all | solution.py:53
  47.2 4.4 %all-to-all-start.1 = ((bf16[4,128,1024]{2,1,0:T(8,128)(2,1)}), bf16[4,128,1024]{2,1,0:T(8,128)(2,1)}, u32[]{:S(2)}, u32[]{:S(2)}) async-start(bf16[4,128,1024]{2,1,0:T(8,128)(2,1)} %bitcast.122), calls=%async_computation.1 | async-start | bytes 2097152 | tf_op jit(solution)/shard_map/all_to_all | solution.py:50
  55.6 2.2 slice.17
  60.2 77.9 %while.10 = (s32[]{:T(128)}, bf16[8,1,32,8,128]{4,2,3,1,0:T(8,128)(2,1)}, s32[8,8,16]{2,1,0:T(8,128)S(1)}, bf16[2,1,32,64,128]{4,3,2,0,1:T(8,128)(2,1)}, s32[8,8...) while((s32[]{:T(128)}, bf16[8,1,32,8,128]{4,2,3,1,0:T(8,128)(2,1)}, ...), condition=%wide.region_5.6_spmd, body=%wide.region_2.5_spmd.sunk | while | flops 428906624 | bytes 34887876 | solution.py:108
  62.7 2.3 fusion.91
  64.9 2.0 fusion.92
  66.9 3.0 %fusion.93 = bf16[8,1,32,8,128]{4,2,3,1,0:T(8,128)(2,1)} fusion(bf16[8,1,32,8,128]{4,2,3,1,0:T(8,128)(2,1)} %get-tuple-element.127, s32[]{:T(128)S(6)} %copy.82, f32[8,128,16,128]{1,3,2,0:T(8,128)S(1)} %get-tuple-element.116, f32[8,128]{1,0:T(8,128)S(1)} %fusion.92, f32[8,128]{1,0:T(8,128)S(1)} %get-tuple-element.117, ...), kind=kOutput, calls=%fused_computation.12.clone.1 | convolution fusion | flops 144736256 | bytes 9511044 | tf_op jit(solution)/shard_map/while/body/eval_jaxpr/qlisj,leqsj->leqi/dot_general | solution.py:103
  70.0 2.0 convert_bitcast_fusion.2
  72.4 2.3 fusion.91
  74.7 2.0 fusion.92
  76.7 3.0 %fusion.93 = bf16[8,1,32,8,128]{4,2,3,1,0:T(8,128)(2,1)} fusion(bf16[8,1,32,8,128]{4,2,3,1,0:T(8,128)(2,1)} %get-tuple-element.127, s32[]{:T(128)S(6)} %copy.82, f32[8,128,16,128]{1,3,2,0:T(8,128)S(1)} %get-tuple-element.116, f32[8,128]{1,0:T(8,128)S(1)} %fusion.92, f32[8,128]{1,0:T(8,128)S(1)} %get-tuple-element.117, ...), kind=kOutput, calls=%fused_computation.12.clone.1 | convolution fusion | flops 144736256 | bytes 9511044 | tf_op jit(solution)/shard_map/while/body/eval_jaxpr/qlisj,leqsj->leqi/dot_general | solution.py:103
  79.7 2.0 convert_bitcast_fusion.2
  82.1 2.3 fusion.91
  84.4 2.0 fusion.92
  86.4 3.0 %fusion.93 = bf16[8,1,32,8,128]{4,2,3,1,0:T(8,128)(2,1)} fusion(bf16[8,1,32,8,128]{4,2,3,1,0:T(8,128)(2,1)} %get-tuple-element.127, s32[]{:T(128)S(6)} %copy.82, f32[8,128,16,128]{1,3,2,0:T(8,128)S(1)} %get-tuple-element.116, f32[8,128]{1,0:T(8,128)S(1)} %fusion.92, f32[8,128]{1,0:T(8,128)S(1)} %get-tuple-element.117, ...), kind=kOutput, calls=%fused_computation.12.clone.1 | convolution fusion | flops 144736256 | bytes 9511044 | tf_op jit(solution)/shard_map/while/body/eval_jaxpr/qlisj,leqsj->leqi/dot_general | solution.py:103
  89.5 2.0 convert_bitcast_fusion.2
  91.9 2.3 fusion.91
  94.1 2.0 fusion.92
  96.1 3.0 %fusion.93 = bf16[8,1,32,8,128]{4,2,3,1,0:T(8,128)(2,1)} fusion(bf16[8,1,32,8,128]{4,2,3,1,0:T(8,128)(2,1)} %get-tuple-element.127, s32[]{:T(128)S(6)} %copy.82, f32[8,128,16,128]{1,3,2,0:T(8,128)S(1)} %get-tuple-element.116, f32[8,128]{1,0:T(8,128)S(1)} %fusion.92, f32[8,128]{1,0:T(8,128)S(1)} %get-tuple-element.117, ...), kind=kOutput, calls=%fused_computation.12.clone.1 | convolution fusion | flops 144736256 | bytes 9511044 | tf_op jit(solution)/shard_map/while/body/eval_jaxpr/qlisj,leqsj->leqi/dot_general | solution.py:103
  99.2 2.0 convert_bitcast_fusion.2
  101.6 2.3 fusion.91
  103.9 2.0 fusion.92
  105.9 3.0 %fusion.93 = bf16[8,1,32,8,128]{4,2,3,1,0:T(8,128)(2,1)} fusion(bf16[8,1,32,8,128]{4,2,3,1,0:T(8,128)(2,1)} %get-tuple-element.127, s32[]{:T(128)S(6)} %copy.82, f32[8,128,16,128]{1,3,2,0:T(8,128)S(1)} %get-tuple-element.116, f32[8,128]{1,0:T(8,128)S(1)} %fusion.92, f32[8,128]{1,0:T(8,128)S(1)} %get-tuple-element.117, ...), kind=kOutput, calls=%fused_computation.12.clone.1 | convolution fusion | flops 144736256 | bytes 9511044 | tf_op jit(solution)/shard_map/while/body/eval_jaxpr/qlisj,leqsj->leqi/dot_general | solution.py:103
  108.9 2.0 convert_bitcast_fusion.2
  111.3 2.3 fusion.91
  113.6 2.0 fusion.92
  115.6 3.0 %fusion.93 = bf16[8,1,32,8,128]{4,2,3,1,0:T(8,128)(2,1)} fusion(bf16[8,1,32,8,128]{4,2,3,1,0:T(8,128)(2,1)} %get-tuple-element.127, s32[]{:T(128)S(6)} %copy.82, f32[8,128,16,128]{1,3,2,0:T(8,128)S(1)} %get-tuple-element.116, f32[8,128]{1,0:T(8,128)S(1)} %fusion.92, f32[8,128]{1,0:T(8,128)S(1)} %get-tuple-element.117, ...), kind=kOutput, calls=%fused_computation.12.clone.1 | convolution fusion | flops 144736256 | bytes 9511044 | tf_op jit(solution)/shard_map/while/body/eval_jaxpr/qlisj,leqsj->leqi/dot_general | solution.py:103
  118.7 2.0 convert_bitcast_fusion.2
  121.1 2.3 fusion.91
  123.3 2.0 fusion.92
  125.3 3.0 %fusion.93 = bf16[8,1,32,8,128]{4,2,3,1,0:T(8,128)(2,1)} fusion(bf16[8,1,32,8,128]{4,2,3,1,0:T(8,128)(2,1)} %get-tuple-element.127, s32[]{:T(128)S(6)} %copy.82, f32[8,128,16,128]{1,3,2,0:T(8,128)S(1)} %get-tuple-element.116, f32[8,128]{1,0:T(8,128)S(1)} %fusion.92, f32[8,128]{1,0:T(8,128)S(1)} %get-tuple-element.117, ...), kind=kOutput, calls=%fused_computation.12.clone.1 | convolution fusion | flops 144736256 | bytes 9511044 | tf_op jit(solution)/shard_map/while/body/eval_jaxpr/qlisj,leqsj->leqi/dot_general | solution.py:103
  130.8 2.3 fusion.91
  133.1 2.0 fusion.92
  135.1 3.0 %fusion.93 = bf16[8,1,32,8,128]{4,2,3,1,0:T(8,128)(2,1)} fusion(bf16[8,1,32,8,128]{4,2,3,1,0:T(8,128)(2,1)} %get-tuple-element.127, s32[]{:T(128)S(6)} %copy.82, f32[8,128,16,128]{1,3,2,0:T(8,128)S(1)} %get-tuple-element.116, f32[8,128]{1,0:T(8,128)S(1)} %fusion.92, f32[8,128]{1,0:T(8,128)S(1)} %get-tuple-element.117, ...), kind=kOutput, calls=%fused_computation.12.clone.1 | convolution fusion | flops 144736256 | bytes 9511044 | tf_op jit(solution)/shard_map/while/body/eval_jaxpr/qlisj,leqsj->leqi/dot_general | solution.py:103
  140.3 2.2 copy.43
  142.5 4.2 %all-to-all-start.3 = ((bf16[32,32,256]{2,0,1:T(8,128)(2,1)}), bf16[32,32,256]{2,0,1:T(8,128)(2,1)S(1)}, u32[]{:S(2)}, u32[]{:S(2)}) async-start(bf16[32,32,256]{2,0,1:T(8,128)(2,1)} %copy.43), calls=%async_computation.3 | async-start | bytes 1048576 | tf_op jit(solution)/shard_map/all_to_all | solution.py:117
  146.7 9.7 %gather_fusion = bf16[2048,1024]{1,0:T(8,128)(2,1)} fusion(bf16[256,1024]{1,0:T(8,128)(2,1)S(1)} %convolution_convert_fusion.2, s32[2048]{0:T(1024)S(1)} %broadcast_clamp_fusion), kind=kCustom, calls=%fused_computation | custom fusion | bytes 8396800 | tf_op jit(solution)/shard_map/gather | solution.py:45
  156.4 2.0 all-to-all-done.3
  158.4 5.7 %all-to-all-start = ((bf16[32,64,1024]{2,1,0:T(8,128)(2,1)}), bf16[32,64,1024]{2,1,0:T(8,128)(2,1)}, u32[]{:S(2)}, u32[]{:S(2)}) async-start(bf16[32,64,1024]{2,1,0:T(8,128)(2,1)} %bitcast.120), calls=%async_computation | async-start | bytes 8388608 | tf_op jit(solution)/shard_map/all_to_all | solution.py:46
  164.2 3.4 %convolution_convert_fusion.1 = bf16[2,22,128,128]{3,1,2,0:T(8,128)(2,1)} fusion(bf16[2,16,128,128]{3,2,1,0:T(8,128)(2,1)} %param.16, s32[2,16]{1,0:T(2,128)S(1)} %copy-done.7), kind=kOutput, calls=%fused_computation.46 | convolution fusion | flops 23790272 | bytes 2490496 | tf_op jit(solution)/shard_map/bst,bsij->bitj/dot_general | solution.py:59
  170.7 45.7 %all-to-all-done = bf16[32,64,1024]{2,1,0:T(8,128)(2,1)} async-done(((bf16[32,64,1024]{2,1,0:T(8,128)(2,1)}), bf16[32,64,1024]{2,1,0:T(8,128)(2,1)}, u32[]{:S(2)}, u32[]{:S(2)}) %all-to-all-start) | async-done | bytes 4194336 | tf_op jit(solution)/shard_map/all_to_all | solution.py:46
  216.3 4.8 %fusion.69 = (f32[256]{0:T(256)S(1)}, f32[256,1024]{1,0:T(8,128)S(1)}) fusion(bf16[512,1024]{1,0:T(8,128)(2,1)} %bitcast.31, bf16[2048,1024]{1,0:T(8,128)(2,1)} %bitcast.27, bf16[256,1024]{1,0:T(8,128)(2,1)S(1)} %convolution_convert_fusion.2, bf16[32,8,22,128]{3,2,1,0:T(8,128)(2,1)} %bitcast.124, bf16[256,1024]{1,0:T(8,128)(2,1)} %param.14), kind=kOutput, calls=%fused_computation.90 | convolution fusion | flops 1494482688 | bytes 8782848 | tf_op jit(solution)/shard_map/dot_general | solution.py:62
  222.1 7.5 %fusion.70 = (f32[256]{0:T(256)S(1)}, f32[256,1024]{1,0:T(8,128)S(1)}) fusion(bf16[2048,1024]{1,0:T(8,128)(2,1)} %param.25, bf16[1024,2048]{1,0:T(8,128)(2,1)} %param.24, f32[256,1024]{1,0:T(8,128)} %copy-done.1, f32[256,1024]{1,0:T(8,128)} %copy-done.2, f32[256]{0:T(256)S(1)} %get-tuple-element.72, f32[256]{0:T(256)S(1)} %broadcast_multiply_fusion.1, ...), kind=kOutput, calls=%fused_computation.91 | convolution fusion | flops 2155609856 | bytes 11539456 | tf_op jit(solution)/shard_map/dot_general | solution.py:127
  (87 shorter events, 23.1 us)
Async XLA Ops:
  0.0 167.5 %copy-start = (bf16[1024,1024]{1,0:T(8,128)(2,1)S(1)}, bf16[1024,1024]{1,0:T(8,128)(2,1)}, u32[]{:S(2)}) copy-start(bf16[1024,1024]{1,0:T(8,128)(2,1)} %param.23) | copy-start | bytes 6291460
  0.0 8.8 %copy-start.3 = (bf16[256,1024]{1,0:T(8,128)(2,1)S(1)}, bf16[256,1024]{1,0:T(8,128)(2,1)}, u32[]{:S(2)}) copy-start(bf16[256,1024]{1,0:T(8,128)(2,1)} %param.14) | copy-start | bytes 1572868
  13.5 11.0 %copy-start.5 = (s32[64,16]{0,1:T(8,128)S(1)}, s32[64,16]{0,1:T(8,128)}, u32[]{:S(2)}) copy-start(s32[64,16]{0,1:T(8,128)} %param.21) | copy-start | bytes 12292
  13.5 11.1 %copy-start.8 = (s32[64]{0:T(128)S(1)}, s32[64]{0:T(128)}, u32[]{:S(2)}) copy-start(s32[64]{0:T(128)} %param.22) | copy-start | bytes 772
  13.5 11.1 %copy-start.4 = (s32[1,32,64]{2,1,0:T(8,128)S(1)}, s32[1,32,64]{2,1,0:T(8,128)}, u32[]{:S(2)}) copy-start(s32[1,32,64]{2,1,0:T(8,128)} %param.18) | copy-start | bytes 24580
  13.5 11.2 %copy-start.6 = (s32[1,4,128]{2,1,0:T(4,128)S(1)}, s32[1,4,128]{2,1,0:T(4,128)}, u32[]{:S(2)}) copy-start(s32[1,4,128]{2,1,0:T(4,128)} %param.19) | copy-start | bytes 6148
  14.8 32.4 %all-to-all-start.2 = ((bf16[32,3,32,256]{3,2,1,0:T(8,128)(2,1)}), bf16[32,3,32,256]{3,2,1,0:T(8,128)(2,1)}, u32[]{:S(2)}, u32[]{:S(2)}) async-start(bf16[32,3,32,256]{3,2,1,0:T(8,128)(2,1)} %copy.38), calls=%async_computation.2 | async-start | bytes 3145728 | tf_op jit(solution)/shard_map/all_to_all | solution.py:53
  47.2 95.3 %all-to-all-start.1 = ((bf16[4,128,1024]{2,1,0:T(8,128)(2,1)}), bf16[4,128,1024]{2,1,0:T(8,128)(2,1)}, u32[]{:S(2)}, u32[]{:S(2)}) async-start(bf16[4,128,1024]{2,1,0:T(8,128)(2,1)} %bitcast.122), calls=%async_computation.1 | async-start | bytes 2097152 | tf_op jit(solution)/shard_map/all_to_all | solution.py:50
  142.5 16.0 %all-to-all-start.3 = ((bf16[32,32,256]{2,0,1:T(8,128)(2,1)}), bf16[32,32,256]{2,0,1:T(8,128)(2,1)S(1)}, u32[]{:S(2)}, u32[]{:S(2)}) async-start(bf16[32,32,256]{2,0,1:T(8,128)(2,1)} %copy.43), calls=%async_computation.3 | async-start | bytes 1048576 | tf_op jit(solution)/shard_map/all_to_all | solution.py:117
  158.4 5.7 %copy-start.7 = (s32[2,16]{1,0:T(2,128)S(1)}, s32[2,16]{1,0:T(2,128)}, u32[]{:S(2)}) copy-start(s32[2,16]{1,0:T(2,128)} %param.17) | copy-start | bytes 388
  158.4 57.9 %all-to-all-start = ((bf16[32,64,1024]{2,1,0:T(8,128)(2,1)}), bf16[32,64,1024]{2,1,0:T(8,128)(2,1)}, u32[]{:S(2)}, u32[]{:S(2)}) async-start(bf16[32,64,1024]{2,1,0:T(8,128)(2,1)} %bitcast.120), calls=%async_computation | async-start | bytes 8388608 | tf_op jit(solution)/shard_map/all_to_all | solution.py:46
  169.4 1.0 copy-start.1
  221.1 1.0 copy-start.2
where the time goes:
time: 233 us; the launch traced here: 231 us
  matrix products  82.3 us (35%)
  waiting for transfers between devices  65 us (28%)
  local copies, waits for them, and re-layouts  40.7 us (17%)
  starting transfers between devices  24 us (10%)
  other arithmetic  18.3 us (8%)
    all_to_all x1, waiting for transfers between devices, per_device(): lax.all_to_all(send_inner, 'dev', split_axis=0, concat_axis=0, tiled=True)  45.7 us
    dot_general x8, matrix products, attend(): jnp.einsum('qlisj,leqsj->leqi', probs, values_here, preferred_element_typ...  24 us
    dot_general x8, matrix products, attend(): jnp.einsum('leqi,leqsj->qlisj', queries, keys_here, preferred_element_typ...  18.2 us
    all_to_all x1, waiting for transfers between devices, per_device(): lax.all_to_all(qkv_split, 'dev', split_axis=0, concat_axis=3, tiled=True)  17.3 us
    reduce_sum x8, other arithmetic, attend(): totals = jnp.sum(expos, axis=(3, 4), keepdims=True)  15.9 us
    dot_general x8, matrix products, attend(): jnp.einsum('qst,kletj->kleqsj', picker, key_value, preferred_element_type...  15.8 us
    unnamed x20, local copies, waits for them, and re-layouts  10.6 us
    gather x1, local copies, waits for them, and re-layouts, per_device(): send_inner = gcn_rows[inner_rows[0].reshape(-1)].reshape(peers, -1, width)  9.71 us
  transfers between devices with their start and end apart: 4, of which 3 were waited for; matrix products, arithmetic and copies ran while one was open for 48% of the time, Pallas kernels for 0%

commit v1 on v0

v1 whole, which is shorter than its diff:
```python
import jax
import jax.numpy as jnp
from jax import lax
from jax.experimental import pallas as pl
from jax.experimental.pallas import tpu as pltpu
from jax.sharding import PartitionSpec as P

MESH = pl.DeviceIdType.MESH
BF = jnp.bfloat16
F32 = jnp.float32
HEADS = 32
HEAD = 32
RING = 4
STEPS = (0, -1, 1, 2)
ONES_LANE = 2 * HEAD


def wrap(v):
    return (v + RING) % RING


def place():
    d = lax.axis_index("dev")
    return d, d // 8, (d // 2) % 4, d % 2


def dev_of(y, z, c):
    return y * 8 + z * 2 + c


def dot(a, b):
    return jnp.dot(a, b, preferred_element_type=F32)


def dot_nt(a, b):
    return lax.dot_general(a, b, (((1,), (1,)), ((), ())), preferred_element_type=F32)


def dot_tn(a, b):
    return lax.dot_general(a, b, (((0,), (0,)), ((), ())), preferred_element_type=F32)


def layer_norm(values):
    average = jnp.mean(values, axis=-1, keepdims=True)
    centered = values - average
    variance = jnp.mean(centered * centered, axis=-1, keepdims=True)
    return centered / jnp.sqrt(variance + 1e-05)


def gather_kernel(
    x_hbm, wg_hbm, wqkv_hbm, inner_ref, outer_ref,
    q_hbm, kv_hbm, tab_hbm,
    xall, idx, wg, w3, wc, xsel, tab, q, kv, outsel,
    send_sem, recv_sem, isend, irecv, sib_send, sib_recv, sibi_send, sibi_recv,
    out_send, out_recv, local_sem, back_sem,
):
    d, y, z, c = place()
    g = lax.axis_index("group")
    sib = dev_of(y, z, 1 - c)
    near = [
        dev_of(wrap(y + 1), z, c), dev_of(wrap(y - 1), z, c),
        dev_of(y, wrap(z + 1), c), dev_of(y, wrap(z - 1), c), sib,
    ]
    bar = pltpu.get_barrier_semaphore()
    for n in near:
        pl.semaphore_signal(bar, inc=1, device_id={"dev": n}, device_id_type=MESH)
    for r in range(1, 4):
        pl.semaphore_signal(bar, inc=1, device_id={"group": wrap(g + r)}, device_id_type=MESH)
    me = y * 4 + z
    loads = [
        pltpu.make_async_copy(x_hbm.at[pl.ds(b * 128, 128)], xall.at[me, c, b], local_sem.at[b])
        for b in range(2)
    ]
    loads.append(pltpu.make_async_copy(wg_hbm, wg, local_sem.at[2]))
    window = pl.multiple_of((d // 4) * 128, 128)
    for t in range(3):
        loads.append(
            pltpu.make_async_copy(
                wqkv_hbm.at[:, pl.ds(t * 1024 + window, 128)], w3.at[t], local_sem.at[3 + t]
            )
        )
    for load in loads:
        load.start()
    idx[me, c, :, 0:64] = inner_ref[0]
    idx[me, c, :, 64:128] = jnp.zeros((32, 64), jnp.int32)
    pl.semaphore_wait(bar, len(near) + 3)
    loads[0].wait()
    loads[1].wait()
    started = []

    class Route:
        def __init__(self, b):
            self.b = b
            self.p, self.s = (y, z) if b == 0 else (z, y)

        def chip(self, dp, ds):
            p, s = wrap(self.p + dp), wrap(self.s + ds)
            return p * 4 + s if self.b == 0 else s * 4 + p

        def target(self, dp, ds):
            p, s = wrap(self.p + dp), wrap(self.s + ds)
            return dev_of(p, s, c) if self.b == 0 else dev_of(s, p, c)

        def view(self, dp, ds, half):
            r = xall.at[self.chip(dp, ds), c, self.b]
            return r if half is None else r.at[pl.ds(half * 64, 64)]

        def copies(self, tag, dp, ds, half, to):
            v = self.view(dp, ds, half)
            k = self.b * 20 + tag
            out = [
                pltpu.make_async_remote_copy(
                    v, v, send_sem.at[k], recv_sem.at[k], device_id={"dev": to}, device_id_type=MESH
                )
            ]
            if self.b == 0 and half != 1:
                v = idx.at[self.chip(dp, ds), c]
                out.append(
                    pltpu.make_async_remote_copy(
                        v, v, isend.at[tag], irecv.at[tag], device_id={"dev": to}, device_id_type=MESH
                    )
                )
            return out

        def send(self, tag, dp, ds, half, to_p, to_s):
            for copy in self.copies(tag, dp, ds, half, self.target(to_p, to_s)):
                copy.start()
                started.append(copy)

        def wait(self, tag, dp, ds, half=None):
            for copy in self.copies(tag, dp, ds, half, sib):
                copy.wait_recv()

        def sib_copy(self, dp, ds):
            i = self.chip(dp, ds)
            v = self.view(dp, ds, None)
            copies = [
                pltpu.make_async_remote_copy(
                    v, v, sib_send.at[i * 2 + self.b], sib_recv.at[i * 2 + self.b],
                    device_id={"dev": sib}, device_id_type=MESH,
                )
            ]
            if self.b == 0:
                v = idx.at[i, c]
                copies.append(
                    pltpu.make_async_remote_copy(
                        v, v, sibi_send.at[i], sibi_recv.at[i],
                        device_id={"dev": sib}, device_id_type=MESH,
                    )
                )
            for copy in copies:
                copy.start()
                started.append(copy)

    def sib_wait(chip):
        for b in range(2):
            v = xall.at[chip, 1 - c, b]
            pltpu.make_async_remote_copy(
                v, v, sib_send.at[chip * 2 + b], sib_recv.at[chip * 2 + b],
                device_id={"dev": sib}, device_id_type=MESH,
            ).wait_recv()
        v = idx.at[chip, 1 - c]
        pltpu.make_async_remote_copy(
            v, v, sibi_send.at[chip], sibi_recv.at[chip],
            device_id={"dev": sib}, device_id_type=MESH,
        ).wait_recv()

    lane = lax.broadcasted_iota(jnp.int32, (256, 128), 1)
    row = lax.broadcasted_iota(jnp.int32, (256, 64), 0)

    def back(k, src, dst):
        return pltpu.make_async_copy(src, dst, back_sem.at[k])

    def backs(chip):
        return [
            back(chip * 3, q.at[pl.ds(chip * 4, 4)], q_hbm.at[pl.ds(chip * 4, 4)]),
            back(chip * 3 + 1, kv.at[pl.ds(chip * 4, 4)], kv_hbm.at[pl.ds(chip * 4, 4)]),
            back(chip * 3 + 2, tab.at[2 + chip], tab_hbm.at[2 + chip]),
        ]

    def process(chip):
        sib_wait(chip)
        for cc in range(2):
            rows = xall[chip, cc].reshape(256, 1024)
            both = dot(rows, wc[...])
            at = chip * 4 + cc * 2
            q[pl.ds(at, 2)] = both[:, :128].astype(BF).reshape(2, 128, 128)
            kv[pl.ds(at, 2)] = (
                jnp.where(lane == ONES_LANE, 1.0, both[:, 128:]).astype(BF).reshape(2, 128, 128)
            )
            picks = idx[chip, cc, pl.ds(d, 1), :][:, 0:64]
            hot = jnp.where(row == picks, 1.0, 0.0).astype(BF)
            xsel[pl.ds(cc * 64, 64), :] = dot_tn(hot, rows).astype(BF)
        tab[2 + chip] = dot(xsel[...], wg[...]).astype(BF)
        for copy in backs(chip):
            copy.start()

    def process_many(count, where):
        def step(i, carry):
            dy, dz = where(i)
            process(wrap(y + dy) * 4 + wrap(z + dz))
            return carry

        lax.fori_loop(0, count, step, 0)

    routes = [Route(0), Route(1)]
    for t in routes:
        t.send(0, 0, 0, None, 1, 0)
        t.send(1, 0, 0, None, -1, 0)
    for t in routes:
        t.send(4, 0, 0, None, 0, 1)
        t.send(5, 0, 0, None, 0, -1)
    for t in routes:
        t.sib_copy(0, 0)

    loads[2].wait()
    own = dot(xall[me, c].reshape(256, 1024), wg[...]).astype(BF)
    tab[0:2] = own.reshape(2, 128, 1024)
    for r in range(4):
        to = wrap(g + r)
        picks = outer_ref[0, pl.ds(to, 1), :]
        hot = jnp.where(
            lax.broadcasted_iota(jnp.int32, (256, 128), 0) == picks, 1.0, 0.0
        ).astype(BF)
        rows = dot_tn(hot, own).astype(BF)
        if r == 0:
            tab[18 + g] = rows
        else:
            outsel[r - 1] = rows
            copy = pltpu.make_async_remote_copy(
                outsel.at[r - 1], tab.at[18 + g], out_send.at[r - 1], out_recv.at[r - 1],
                device_id={"group": to}, device_id_type=MESH,
            )
            copy.start()
            started.append(copy)

    for t in range(3):
        loads[3 + t].wait()
    take = lax.broadcasted_iota(jnp.int32, (128, 256), 0) - (d % 4) * HEAD
    col = lax.broadcasted_iota(jnp.int32, (128, 256), 1)
    total = jnp.zeros((1024, 256), F32)
    for t in range(3):
        first = (0, 128, 128 + HEAD)[t]
        inside = (take >= 0) & (take < HEAD) & (col == take + first)
        total = total + dot(w3[t], jnp.where(inside, 1.0, 0.0).astype(BF))
    wc[...] = total.astype(BF)

    def e1():
        for t in routes:
            t.wait(0, -1, 0)
            t.send(2, -1, 0, 0, 1, 0)
            t.wait(1, 1, 0)
            t.send(3, 1, 0, 1, -1, 0)
        for t in routes:
            for k in (1, 2):
                t.send(4 + 4 * k, STEPS[k], 0, None, 0, 1)
                t.send(5 + 4 * k, STEPS[k], 0, None, 0, -1)
                t.sib_copy(STEPS[k], 0)

    def e2():
        for t in routes:
            t.wait(2, 2, 0, 0)
            t.wait(3, 2, 0, 1)
            t.send(16, 2, 0, None, 0, 1)
            t.send(17, 2, 0, None, 0, -1)
            t.sib_copy(2, 0)

    def e3(k):
        for t in routes:
            t.wait(4 + 4 * k, STEPS[k], -1)
            t.send(6 + 4 * k, STEPS[k], -1, 0, 0, 1)
            t.wait(5 + 4 * k, STEPS[k], 1)
            t.send(7 + 4 * k, STEPS[k], 1, 1, 0, -1)
            t.sib_copy(STEPS[k], -1)
            t.sib_copy(STEPS[k], 1)

    def e4(k):
        for t in routes:
            t.wait(6 + 4 * k, STEPS[k], 2, 0)
            t.wait(7 + 4 * k, STEPS[k], 2, 1)
            t.sib_copy(STEPS[k], 2)

    def sign(i):
        return 1 - 2 * (i % 2)

    e1()
    process_many(1, lambda i: (0 * i, 0 * i))
    e2()
    e3(0)
    process_many(2, lambda i: (sign(i), 0 * i))
    e3(1)
    e4(0)
    process_many(
        4,
        lambda i: (
            (i // 2) * 2 * (i % 2),
            sign(i) * (1 - i // 2) + (i // 2) * 2 * (1 - i % 2),
        ),
    )
    e3(2)
    e4(1)
    process_many(4, lambda i: (sign(i), 1 - 2 * (i // 2)))
    e3(3)
    e4(2)
    process_many(
        4,
        lambda i: (
            sign(i) * (1 - i // 2) + 2 * (i // 2),
            sign(i) * (i // 2) + 2 * (1 - i // 2),
        ),
    )
    e4(3)
    process_many(1, lambda i: (2 + 0 * i, 2 + 0 * i))

    for r in range(1, 4):
        pltpu.make_async_remote_copy(
            outsel.at[r - 1], tab.at[18 + wrap(g - r)], out_send.at[r - 1], out_recv.at[r - 1],
            device_id={"group": wrap(g + r)}, device_id_type=MESH,
        ).wait_recv()
    kv[64] = jnp.zeros((128, 128), BF)
    tails = [
        back(48, tab.at[pl.ds(0, 2)], tab_hbm.at[pl.ds(0, 2)]),
        back(49, tab.at[pl.ds(18, 4)], tab_hbm.at[pl.ds(18, 4)]),
        back(50, kv.at[64], kv_hbm.at[64]),
    ]
    for copy in tails:
        copy.start()
    for copy in started:
        copy.wait_send()
    for chip in range(16):
        for copy in backs(chip):
            copy.wait()
    for copy in tails:
        copy.wait()


def attend_kernel(blocks, counts, q_ref, kv_ref, o_ref, s_ref):
    factor = 1.4426950408889634 / HEAD**0.5
    dead = kv_ref.shape[0] - 1

    def one(i, lanes, slots):
        query = q_ref[i]
        count = counts[i]
        first = blocks[i, 0]
        highest = None
        for s in range(slots):
            at = jnp.where(s < count, blocks[i, s], first)
            scores = dot_nt(query, kv_ref[at])
            s_ref[s] = scores
            highest = scores if highest is None else jnp.maximum(highest, scores)
        top = jnp.max(highest, axis=1, keepdims=True) * factor
        mixed = None
        for s in range(slots):
            at = jnp.where(s < count, blocks[i, s], dead)
            probs = jnp.exp2(s_ref[s] * factor - top).astype(BF)
            part = dot(probs, kv_ref[at])
            mixed = part if mixed is None else mixed + part
        turned = mixed.T
        part = turned[HEAD : 2 * HEAD] / turned[ONES_LANE : ONES_LANE + 1]
        o_ref[i // 2, :, lanes * 128 : lanes * 128 + 128] = part.astype(BF)

    def step(j, carry):
        for lanes in range(2):
            i = 2 * j + lanes
            fours = (counts[i] + 3) // 4
            for n in range(1, 5):
                @pl.when(fours == n)
                def _():
                    one(i, lanes, 4 * n)
        return carry

    lax.fori_loop(0, q_ref.shape[0] // 2, step, 0)


def finish_kernel(
    ot, tab_hbm, adj_hbm, nb_ref, x_ref, wo_hbm, wu_hbm, wd_hbm,
    o_ref,
    ret, tab, adj, wo, wu, wd, summed,
    send_sem, recv_sem, local_sem,
):
    d, y, z, c = place()
    loads = [
        pltpu.make_async_copy(src, dst, local_sem.at[i])
        for i, (src, dst) in enumerate(
            ((adj_hbm, adj), (tab_hbm, tab), (wo_hbm, wo), (wu_hbm, wu), (wd_hbm, wd), (ot.at[d], ret.at[d]))
        )
    ]
    bar = pltpu.get_barrier_semaphore()

    def other(r):
        return dev_of(wrap(y + r // 8), wrap(z + (r // 2) % 4), (c + r % 2) % 2)

    def source(r):
        return dev_of(wrap(y - r // 8), wrap(z - (r // 2) % 4), (c + r % 2) % 2)

    def hail(r, carry):
        pl.semaphore_signal(bar, inc=1, device_id={"dev": other(r)}, device_id_type=MESH)
        return carry

    lax.fori_loop(1, 32, hail, 0)
    for load in loads:
        load.start()
    pl.semaphore_wait(bar, 31)

    def copy(r):
        return pltpu.make_async_remote_copy(
            ot.at[other(r)], ret.at[d], send_sem.at[r], recv_sem.at[r],
            device_id={"dev": other(r)}, device_id_type=MESH,
        )

    def arrive(r):
        return pltpu.make_async_remote_copy(
            ot.at[other(r)], ret.at[source(r)], send_sem.at[r], recv_sem.at[r],
            device_id={"dev": other(r)}, device_id_type=MESH,
        )

    def push(r, carry):
        copy(r).start()
        return carry

    lax.fori_loop(1, 32, push, 0)
    loads[0].wait()
    loads[1].wait()
    for b in range(2):
        total = None
        for s in range(16):
            part = dot(adj[b, s], tab[nb_ref[b, s]])
            total = part if total is None else total + part
        features = x_ref[pl.ds(b * 128, 128), :].astype(F32)
        summed[pl.ds(b * 128, 128), :] = layer_norm(features + total)
    loads[2].wait()
    loads[5].wait()

    def land(r, carry):
        arrive(r).wait_recv()
        return carry

    lax.fori_loop(1, 32, land, 0)
    projected = dot_tn(ret[...].reshape(1024, 256), wo[...])
    both = summed[...] + layer_norm(x_ref[...].astype(F32) + projected)
    summed[...] = both
    loads[3].wait()
    hidden = jax.nn.gelu(dot(both.astype(BF), wu[...])).astype(BF)
    loads[4].wait()
    o_ref[...] = layer_norm(summed[...] + dot(hidden, wd[...])).astype(BF)

    def leave(r, carry):
        copy(r).wait_send()
        return carry

    lax.fori_loop(1, 32, leave, 0)


def per_device(
    node_feats, w_gcn, adj_tiles, neighbor_blocks, inner_rows, outer_rows,
    w_qkv, key_blocks, key_counts, w_out, w_up, w_down,
):
    hbm = pl.BlockSpec(memory_space=pl.ANY)
    vmem = pl.BlockSpec(memory_space=pltpu.VMEM)
    smem = pl.BlockSpec(memory_space=pltpu.SMEM)
    dma = pltpu.SemaphoreType.DMA
    q, kv, tab = pl.pallas_call(
        gather_kernel,
        out_shape=(
            jax.ShapeDtypeStruct((64, 128, 128), BF),
            jax.ShapeDtypeStruct((65, 128, 128), BF),
            jax.ShapeDtypeStruct((22, 128, 1024), BF),
        ),
        in_specs=[hbm, hbm, hbm, vmem, vmem],
        out_specs=(hbm, hbm, hbm),
        scratch_shapes=[
            pltpu.VMEM((16, 2, 2, 128, 1024), BF),
            pltpu.VMEM((16, 2, 32, 128), jnp.int32),
            pltpu.VMEM((1024, 1024), BF),
            pltpu.VMEM((3, 1024, 128), BF),
            pltpu.VMEM((1024, 256), BF),
            pltpu.VMEM((128, 1024), BF),
            pltpu.VMEM((22, 128, 1024), BF),
            pltpu.VMEM((64, 128, 128), BF),
            pltpu.VMEM((65, 128, 128), BF),
            pltpu.VMEM((3, 128, 1024), BF),
            dma((40,)), dma((40,)), dma((20,)), dma((20,)), dma((32,)), dma((32,)), dma((16,)), dma((16,)),
            dma((3,)), dma((3,)), dma((6,)), dma((51,)),
        ],
        compiler_params=pltpu.CompilerParams(
            collective_id=0, has_side_effects=True, vmem_limit_bytes=48 << 20
        ),
        name="gather",
    )(node_feats, w_gcn, w_qkv, inner_rows, outer_rows)
    ot = pl.pallas_call(
        attend_kernel,
        out_shape=jax.ShapeDtypeStruct((32, 32, 256), BF),
        in_specs=[smem, smem, vmem, vmem],
        out_specs=vmem,
        scratch_shapes=[pltpu.VMEM((16, 128, 128), F32)],
        compiler_params=pltpu.CompilerParams(vmem_limit_bytes=32 << 20),
        name="attend",
    )(key_blocks, key_counts, q, kv)
    return pl.pallas_call(
        finish_kernel,
        out_shape=jax.ShapeDtypeStruct((256, 1024), BF),
        in_specs=[hbm, hbm, hbm, smem, vmem, hbm, hbm, hbm],
        out_specs=vmem,
        scratch_shapes=[
            pltpu.VMEM((32, 32, 256), BF),
            pltpu.VMEM((22, 128, 1024), BF),
            pltpu.VMEM((2, 16, 128, 128), BF),
            pltpu.VMEM((1024, 1024), BF),
            pltpu.VMEM((1024, 2048), BF),
            pltpu.VMEM((2048, 1024), BF),
            pltpu.VMEM((256, 1024), F32),
            dma((32,)), dma((32,)), dma((6,)),
        ],
        compiler_params=pltpu.CompilerParams(
            collective_id=1, has_side_effects=True, vmem_limit_bytes=48 << 20
        ),
        name="finish",
    )(ot, tab, adj_tiles, neighbor_blocks, node_feats, w_out, w_up, w_down)


def solution(mesh):
    placed = (
        P(("group", "dev"), None),
        P(),
        P(("group", "dev"), None, None, None),
        P(("group", "dev"), None),
        P(("group", "dev"), None, None),
        P(("group", "dev"), None, None),
        P(),
        P("group", None),
        P("group"),
        P(),
        P(),
        P(),
    )
    return jax.shard_map(
        per_device, mesh=mesh, in_specs=placed, out_specs=P(("group", "dev"), None), check_vma=False
    )
```

time: 233 us -> 154 us (0.66)
  Pallas kernels: 0 us -> 146 us
  matrix products: 82.3 us -> 0 us
  waiting for transfers between devices: 65 us -> 0 us
  local copies, waits for them, and re-layouts: 40.7 us -> 7.22 us
  starting transfers between devices: 24 us -> 0 us
  other arithmetic: 18.3 us -> 0 us
    pallas_call x0 -> x3, Pallas kernels: none -> 146 us  [the longest x1 70.4 us: per_device(): pl.pallas_call(gather_kernel, out_shape=(jax.ShapeDtypeStruct((64, 128, 1...]
    dot_general x30 -> x0, matrix products: 82.3 us -> none  [the longest x8 24 us: attend(): jnp.einsum('qlisj,leqsj->leqi', probs, values_here, preferred_element_typ...]
    all_to_all x4 -> x0, waiting for transfers between devices: 65 us -> none  [the longest x1 45.7 us: per_device(): lax.all_to_all(send_inner, 'dev', split_axis=0, concat_axis=0, tiled=True)]
    all_to_all x4 -> x0, starting transfers between devices: 24 us -> none  [the longest x1 9.65 us: per_device(): lax.all_to_all(qkv_split, 'dev', split_axis=0, concat_axis=3, tiled=True)]
    reduce_sum x11 -> x0, other arithmetic: 16.7 us -> none  [the longest x8 15.9 us: attend(): totals = jnp.sum(expos, axis=(3, 4), keepdims=True)]
    gather x2 -> x0, local copies, waits for them, and re-layouts: 12.5 us -> none  [the longest x1 9.71 us: per_device(): send_inner = gcn_rows[inner_rows[0].reshape(-1)].reshape(peers, -1, width)]
    slice x5 -> x0, local copies, waits for them, and re-layouts: 7.32 us -> none  [the longest x3 5.13 us: per_device(): key_value = head_parts[1:3]]
    another operation x10 -> x0, local copies, waits for them, and re-layouts: 4.2 us -> none
  transfers between devices with their start and end apart: 4 -> 0, of which waited for: 3 -> 0; matrix products, arithmetic and copies ran while one was open for 48% -> 0% of each run, Pallas kernels for 0% -> 0%
where the time goes in v1:
time: 154 us
  Pallas kernels  146 us (95%)
  local copies, waits for them, and re-layouts  7.22 us (5%)
    pallas_call x1, Pallas kernels, per_device(): pl.pallas_call(gather_kernel, out_shape=(jax.ShapeDtypeStruct((64, 128, 1...  70.4 us
    pallas_call x1, Pallas kernels, per_device(): pl.pallas_call(attend_kernel, out_shape=jax.ShapeDtypeStruct((32, 32, 256...  56.7 us
    pallas_call x1, Pallas kernels, per_device(): pl.pallas_call(finish_kernel, out_shape=jax.ShapeDtypeStruct((256, 1024),...  19.4 us
    unnamed x20, local copies, waits for them, and re-layouts  7.22 us

profile of v1, /device:TPU:1, one launch (start us, length us, event | category | flops | bytes accessed | tf_op | source)
XLA Modules:
  0.0 153.8 jit_solution(15646563579277150860)
XLA Ops:
  0.0 0.8 copy.13.blocks
  0.8 0.0 copy-start.1
  0.8 1.6 %copy-done.1 = bf16[1024,1024]{1,0:T(8,128)(2,1)S(1)} copy-done((bf16[1024,1024]{1,0:T(8,128)(2,1)S(1)}, bf16[1024,1024]{1,0:T(8,128)(2,1)}, u32[]{:S(2)}) %copy-start.1) | copy-done | bytes 2097176
  2.4 0.0 copy-start.3
  2.4 1.0 copy-done.3
  3.4 0.0 copy-start.5
  3.4 0.7 copy-done.5
  4.1 0.0 copy-start.6
  4.1 0.7 copy-done.6
  4.8 0.0 copy-start.8
  4.8 0.0 copy-start.2
  4.8 0.0 copy-start.4
  4.8 70.4 %gather.1 = (bf16[64,128,128]{2,1,0:T(8,128)(2,1)S(1)}, bf16[65,128,128]{2,1,0:T(8,128)(2,1)}, bf16[22,128,1024]{2,1,0:T(8,128)(2,1)}) custom-call(bf16[256,1024]{1,0:T(8,128)(2,1)S(1)} %copy-done.3, bf16[1024,1024]{1,0:T(8,128)(2,1)S(1)} %copy-done.1, bf16[1024,3072]{1,0:T(8,128)(2,1)} %wqkv_hbm.1, s32[1,32,64]{2,1,0:T(8,128)S(1)} %copy-done.5, ...), custom_call_target="tpu_custom_call" | custom-call | tf_op jit(solution)/shard_map/gather/pallas_call | solution.py:462
  75.2 0.0 copy-start.7
  75.2 0.0 copy-done.8
  75.2 0.0 copy-start
  75.2 1.6 %copy-done = bf16[65,128,128]{2,1,0:T(8,128)(2,1)S(1)} copy-done((bf16[65,128,128]{2,1,0:T(8,128)(2,1)S(1)}, bf16[65,128,128]{2,1,0:T(8,128)(2,1)}, u32[]{:S(2)}) %copy-start) | copy-done | bytes 2129944
  76.8 56.7 %attend.1.ot = bf16[32,32,256]{2,1,0:T(8,128)(2,1)S(1)} custom-call(s32[64,16]{1,0:T(8,128)S(1)} %copy.13.blocks, s32[64]{0:T(128)S(1)} %copy-done.8, bf16[64,128,128]{2,1,0:T(8,128)(2,1)S(1)} %get-tuple-element.8.q_ref, bf16[65,128,128]{2,1,0:T(8,128)(2,1)S(1)} %copy-done), custom_call_target="tpu_custom_call" | custom-call | tf_op jit(solution)/shard_map/attend/pallas_call | solution.py:490
  133.6 0.0 copy-done.2
  133.6 0.0 copy-done.4
  133.6 0.0 copy-done.7
  133.6 19.4 %finish.1 = bf16[256,1024]{1,0:T(8,128)(2,1)S(1)} custom-call(bf16[32,32,256]{2,1,0:T(8,128)(2,1)S(1)} %attend.1.ot, bf16[22,128,1024]{2,1,0:T(8,128)(2,1)} %get-tuple-element.10.tab_hbm, bf16[2,16,128,128]{3,2,1,0:T(8,128)(2,1)S(1)} %copy-done.4, s32[2,16]{1,0:T(2,128)S(1)} %copy-done.7, bf16[256,1024]{1,0:T(8,128)(2,1)S(1)} %copy-done.3, ...), custom_call_target="tpu_custom_call" | custom-call | tf_op jit(solution)/shard_map/finish/pallas_call | solution.py:499
  153.0 0.8 copy.15
Async XLA Ops:
  0.8 1.6 %copy-start.1 = (bf16[1024,1024]{1,0:T(8,128)(2,1)S(1)}, bf16[1024,1024]{1,0:T(8,128)(2,1)}, u32[]{:S(2)}) copy-start(bf16[1024,1024]{1,0:T(8,128)(2,1)} %wg_hbm.1) | copy-start | bytes 6291460
  2.4 1.0 copy-start.3
  3.4 0.7 copy-start.5
  4.1 0.7 copy-start.6
  4.8 70.4 %copy-start.8 = (s32[64]{0:T(128)S(1)}, s32[64]{0:T(128)}, u32[]{:S(2)}) copy-start(s32[64]{0:T(128)} %counts.1) | copy-start | bytes 772
  4.8 128.7 %copy-start.2 = (bf16[1024,1024]{1,0:T(8,128)(2,1)S(1)}, bf16[1024,1024]{1,0:T(8,128)(2,1)}, u32[]{:S(2)}) copy-start(bf16[1024,1024]{1,0:T(8,128)(2,1)} %wo_hbm.1) | copy-start | bytes 6291460
  4.8 128.8 %copy-start.4 = (bf16[2,16,128,128]{3,2,1,0:T(8,128)(2,1)S(1)}, bf16[2,16,128,128]{3,2,1,0:T(8,128)(2,1)}, u32[]{:S(2)}) copy-start(bf16[2,16,128,128]{3,2,1,0:T(8,128)(2,1)} %adj_hbm.1) | copy-start | bytes 3145732
  75.2 58.4 %copy-start.7 = (s32[2,16]{1,0:T(2,128)S(1)}, s32[2,16]{1,0:T(2,128)}, u32[]{:S(2)}) copy-start(s32[2,16]{1,0:T(2,128)} %nb_ref.1) | copy-start | bytes 388
  75.2 1.6 %copy-start = (bf16[65,128,128]{2,1,0:T(8,128)(2,1)S(1)}, bf16[65,128,128]{2,1,0:T(8,128)(2,1)}, u32[]{:S(2)}) copy-start(bf16[65,128,128]{2,1,0:T(8,128)(2,1)} %get-tuple-element.9.kv_ref) | copy-start | bytes 6389764

commit v2 on v1

--- a/solution.py
+++ b/solution.py
@@ -334,42 +334,74 @@
         copy.wait()
 
 
-def attend_kernel(blocks, counts, q_ref, kv_ref, o_ref, s_ref):
+def attend_kernel(blocks, counts, q_ref, kv_ref, o_ref, s_a, s_b, m_a, m_b, order):
     factor = 1.4426950408889634 / HEAD**0.5
     dead = kv_ref.shape[0] - 1
-
-    def one(i, lanes, slots):
+    total = q_ref.shape[0]
+
+    def tally(i, have):
+        fours = (counts[i] + 3) // 4
+        return tuple(h + jnp.where(fours == n + 1, 1, 0) for n, h in enumerate(have))
+
+    have = lax.fori_loop(0, total, tally, (jnp.int32(0),) * 4)
+    first = (jnp.int32(0), have[0], have[0] + have[1], have[0] + have[1] + have[2])
+
+    def enlist(i, at):
+        fours = (counts[i] + 3) // 4
+        where = at[3]
+        for n in range(3):
+            where = jnp.where(fours == n + 1, at[n], where)
+        order[where] = i
+        return tuple(a + jnp.where(fours == n + 1, 1, 0) for n, a in enumerate(at))
+
+    lax.fori_loop(0, total, enlist, first)
+
+    def score(i, slots, scores, tops):
         query = q_ref[i]
-        count = counts[i]
-        first = blocks[i, 0]
         highest = None
-        for s in range(slots):
-            at = jnp.where(s < count, blocks[i, s], first)
-            scores = dot_nt(query, kv_ref[at])
-            s_ref[s] = scores
-            highest = scores if highest is None else jnp.maximum(highest, scores)
-        top = jnp.max(highest, axis=1, keepdims=True) * factor
+        for s in range(0, slots, 2):
+            keys = [
+                kv_ref[jnp.where(s + u < counts[i], blocks[i, s + u], blocks[i, 0])] for u in range(2)
+            ]
+            part = dot_nt(query, jnp.concatenate(keys, axis=0))
+            scores[:, pl.ds(s * 128, 256)] = part
+            part = jnp.maximum(part[:, :128], part[:, 128:])
+            highest = part if highest is None else jnp.maximum(highest, part)
+        tops[...] = jnp.broadcast_to(jnp.max(highest, axis=1, keepdims=True) * factor, (128, 128))
+
+    def mix(i, slots, scores, tops):
+        top = jnp.concatenate([tops[...]] * 2, axis=1)
         mixed = None
-        for s in range(slots):
-            at = jnp.where(s < count, blocks[i, s], dead)
-            probs = jnp.exp2(s_ref[s] * factor - top).astype(BF)
-            part = dot(probs, kv_ref[at])
+        for s in range(0, slots, 2):
+            probs = jnp.exp2(scores[:, pl.ds(s * 128, 256)] * factor - top).astype(BF)
+            values = [
+                kv_ref[jnp.where(s + u < counts[i], blocks[i, s + u], dead)] for u in range(2)
+            ]
+            part = dot(probs, jnp.concatenate(values, axis=0))
             mixed = part if mixed is None else mixed + part
         turned = mixed.T
         part = turned[HEAD : 2 * HEAD] / turned[ONES_LANE : ONES_LANE + 1]
-        o_ref[i // 2, :, lanes * 128 : lanes * 128 + 128] = part.astype(BF)
-
-    def step(j, carry):
-        for lanes in range(2):
-            i = 2 * j + lanes
-            fours = (counts[i] + 3) // 4
-            for n in range(1, 5):
-                @pl.when(fours == n)
-                def _():
-                    one(i, lanes, 4 * n)
-        return carry
-
-    lax.fori_loop(0, q_ref.shape[0] // 2, step, 0)
+        o_ref[i // 2, :, pl.ds(pl.multiple_of((i % 2) * 128, 128), 128)] = part.astype(BF)
+
+    for n in range(4):
+        slots = 4 * n + 4
+        count, start = have[n], first[n]
+
+        def item(t):
+            return order[start + jnp.minimum(t, count - 1)]
+
+        @pl.when(count > 0)
+        def _():
+            score(item(0), slots, s_a, m_a)
+
+            def step(t, carry):
+                score(item(2 * t + 1), slots, s_b, m_b)
+                mix(item(2 * t), slots, s_a, m_a)
+                score(item(2 * t + 2), slots, s_a, m_a)
+                mix(item(2 * t + 1), slots, s_b, m_b)
+                return carry
+
+            lax.fori_loop(0, (count + 1) // 2, step, 0)
 
 
 def finish_kernel(
@@ -483,7 +515,7 @@
             dma((3,)), dma((3,)), dma((6,)), dma((51,)),
         ],
         compiler_params=pltpu.CompilerParams(
-            collective_id=0, has_side_effects=True, vmem_limit_bytes=48 << 20
+            collective_id=0, has_side_effects=True, vmem_limit_bytes=58 << 20
         ),
         name="gather",
     )(node_feats, w_gcn, w_qkv, inner_rows, outer_rows)
@@ -492,7 +524,13 @@
         out_shape=jax.ShapeDtypeStruct((32, 32, 256), BF),
         in_specs=[smem, smem, vmem, vmem],
         out_specs=vmem,
-        scratch_shapes=[pltpu.VMEM((16, 128, 128), F32)],
+        scratch_shapes=[
+            pltpu.VMEM((128, 2048), F32),
+            pltpu.VMEM((128, 2048), F32),
+            pltpu.VMEM((128, 128), F32),
+            pltpu.VMEM((128, 128), F32),
+            pltpu.SMEM((64,), jnp.int32),
+        ],
         compiler_params=pltpu.CompilerParams(vmem_limit_bytes=32 << 20),
         name="attend",
     )(key_blocks, key_counts, q, kv)
@@ -512,7 +550,7 @@
             dma((32,)), dma((32,)), dma((6,)),
         ],
         compiler_params=pltpu.CompilerParams(
-            collective_id=1, has_side_effects=True, vmem_limit_bytes=48 << 20
+            collective_id=1, has_side_effects=True, vmem_limit_bytes=58 << 20
         ),
         name="finish",
     )(ot, tab, adj_tiles, neighbor_blocks, node_feats, w_out, w_up, w_down)

time: 154 us -> 124 us (0.81)
  Pallas kernels: 146 us -> 117 us
    pallas_call x1, Pallas kernels: 56.7 us -> 27.3 us  [per_device(): pl.pallas_call(attend_kernel, out_shape=jax.ShapeDtypeStruct((32, 32, 256...]
    unnamed x20 -> x10, local copies, waits for them, and re-layouts: 7.22 us -> 6.62 us
where the time goes in v2:
time: 124 us
  Pallas kernels  117 us (94%)
  local copies, waits for them, and re-layouts  6.62 us (5%)
    pallas_call x1, Pallas kernels, per_device(): pl.pallas_call(gather_kernel, out_shape=(jax.ShapeDtypeStruct((64, 128, 1...  68.9 us
    pallas_call x1, Pallas kernels, per_device(): pl.pallas_call(attend_kernel, out_shape=jax.ShapeDtypeStruct((32, 32, 256...  27.3 us
    pallas_call x1, Pallas kernels, per_device(): pl.pallas_call(finish_kernel, out_shape=jax.ShapeDtypeStruct((256, 1024),...  20.8 us
    unnamed x10, local copies, waits for them, and re-layouts  6.62 us

profile of v2, /device:TPU:1, one launch (start us, length us, event | category | flops | bytes accessed | tf_op | source)
XLA Modules:
  0.0 123.7 jit_solution(5583050772510180588)
XLA Ops:
  0.0 0.8 copy.13.blocks
  0.8 0.0 copy-start.3
  0.8 68.9 %gather.1 = (bf16[64,128,128]{2,1,0:T(8,128)(2,1)}, bf16[65,128,128]{2,1,0:T(8,128)(2,1)}, bf16[22,128,1024]{2,1,0:T(8,128)(2,1)}) custom-call(bf16[256,1024]{1,0:T(8,128)(2,1)} %x_ref.1, bf16[1024,1024]{1,0:T(8,128)(2,1)} %wg_hbm.1, bf16[1024,3072]{1,0:T(8,128)(2,1)} %wqkv_hbm.1, s32[1,32,64]{2,1,0:T(8,128)} %inner_ref.1, s32[1,4,128]{2,1,0:T(4,128)} %outer_ref.1), custom_call_target="tpu_custom_call" | custom-call | tf_op jit(solution)/shard_map/gather/pallas_call | solution.py:494
  69.7 0.0 copy-done.3
  69.7 0.0 copy-start
  69.7 1.6 %copy-done = bf16[65,128,128]{2,1,0:T(8,128)(2,1)S(1)} copy-done((bf16[65,128,128]{2,1,0:T(8,128)(2,1)S(1)}, bf16[65,128,128]{2,1,0:T(8,128)(2,1)}, u32[]{:S(2)}) %copy-start) | copy-done | bytes 2129944
  71.3 0.0 copy-start.2
  71.3 1.6 %copy-done.2 = bf16[64,128,128]{2,1,0:T(8,128)(2,1)S(1)} copy-done((bf16[64,128,128]{2,1,0:T(8,128)(2,1)S(1)}, bf16[64,128,128]{2,1,0:T(8,128)(2,1)}, u32[]{:S(2)}) %copy-start.2) | copy-done | bytes 2097176
  72.9 27.3 %attend.1.ot = bf16[32,32,256]{2,1,0:T(8,128)(2,1)S(1)} custom-call(s32[64,16]{1,0:T(8,128)S(1)} %copy.13.blocks, s32[64]{0:T(128)S(1)} %copy-done.3, bf16[64,128,128]{2,1,0:T(8,128)(2,1)S(1)} %copy-done.2, bf16[65,128,128]{2,1,0:T(8,128)(2,1)S(1)} %copy-done), custom_call_target="tpu_custom_call" | custom-call | tf_op jit(solution)/shard_map/attend/pallas_call | solution.py:522
  100.2 0.0 copy-start.1
  100.2 0.8 copy-done.1
  101.0 20.8 %finish.1 = bf16[256,1024]{1,0:T(8,128)(2,1)} custom-call(bf16[32,32,256]{2,1,0:T(8,128)(2,1)} %copy-done.1, bf16[22,128,1024]{2,1,0:T(8,128)(2,1)} %get-tuple-element.10.tab_hbm, bf16[2,16,128,128]{3,2,1,0:T(8,128)(2,1)} %adj_hbm.1, s32[2,16]{1,0:T(2,128)} %nb_ref.1, bf16[256,1024]{1,0:T(8,128)(2,1)} %x_ref.1, bf16[1024,1024]{1,0:T(8,128)(2,1)} %wo_hbm.1, ...), custom_call_target="tpu_custom_call" | custom-call | tf_op jit(solution)/shard_map/finish/pallas_call | solution.py:537
  121.8 1.9 %copy.15 = bf16[256,1024]{1,0:T(8,128)(2,1)} copy(bf16[256,1024]{1,0:T(8,128)(2,1)} %finish.1) | data formatting | bytes 1048576
Async XLA Ops:
  0.8 68.9 %copy-start.3 = (s32[64]{0:T(128)S(1)}, s32[64]{0:T(128)}, u32[]{:S(2)}) copy-start(s32[64]{0:T(128)} %counts.1) | copy-start | bytes 772
  69.7 1.6 %copy-start = (bf16[65,128,128]{2,1,0:T(8,128)(2,1)S(1)}, bf16[65,128,128]{2,1,0:T(8,128)(2,1)}, u32[]{:S(2)}) copy-start(bf16[65,128,128]{2,1,0:T(8,128)(2,1)} %get-tuple-element.9.kv_ref) | copy-start | bytes 6389764
  71.3 1.6 %copy-start.2 = (bf16[64,128,128]{2,1,0:T(8,128)(2,1)S(1)}, bf16[64,128,128]{2,1,0:T(8,128)(2,1)}, u32[]{:S(2)}) copy-start(bf16[64,128,128]{2,1,0:T(8,128)(2,1)} %get-tuple-element.8.q_ref) | copy-start | bytes 6291460
  100.2 0.8 copy-start.1

commit v3 on v2

v3 whole, which is shorter than its diff:
```python
import jax
import jax.numpy as jnp
from jax import lax
from jax.experimental import pallas as pl
from jax.experimental.pallas import tpu as pltpu
from jax.sharding import PartitionSpec as P

MESH = pl.DeviceIdType.MESH
BF = jnp.bfloat16
F32 = jnp.float32
HEADS = 32
HEAD = 32
RING = 4
STEPS = (0, -1, 1, 2)
ONES_LANE = 2 * HEAD


def wrap(v):
    return (v + RING) % RING


def place():
    d = lax.axis_index("dev")
    return d, d // 8, (d // 2) % 4, d % 2


def dev_of(y, z, c):
    return y * 8 + z * 2 + c


def dot(a, b):
    return jnp.dot(a, b, preferred_element_type=F32)


def dot_nt(a, b):
    return lax.dot_general(a, b, (((1,), (1,)), ((), ())), preferred_element_type=F32)


def dot_tn(a, b):
    return lax.dot_general(a, b, (((0,), (0,)), ((), ())), preferred_element_type=F32)


def layer_norm(values):
    average = jnp.mean(values, axis=-1, keepdims=True)
    centered = values - average
    variance = jnp.mean(centered * centered, axis=-1, keepdims=True)
    return centered / jnp.sqrt(variance + 1e-05)


def layer_kernel(
    x_hbm, wg_hbm, wqkv_hbm, inner_hbm, outer_hbm, adj_hbm, nb_hbm, blocks_hbm, counts_hbm,
    wo_hbm, wu_hbm, wd_hbm,
    o_ref,
    xall, idx, wg, w3, wc, xsel, q, kv, outsel, outin, inner_ref, outer_ref, adj, acc,
    wo, wu, wd, ob, ret, s_a, s_b, m_a, m_b, nb, blocks, counts,
    send_sem, recv_sem, isend, irecv, sib_send, sib_recv, sibi_send, sibi_recv,
    out_send, out_recv, local_sem, ret_send, ret_recv,
):
    d, y, z, c = place()
    g = lax.axis_index("group")
    sib = dev_of(y, z, 1 - c)
    bar = pltpu.get_barrier_semaphore()

    def other(r):
        return dev_of(wrap(y + r // 8), wrap(z + (r // 2) % 4), (c + r % 2) % 2)

    def source(r):
        return dev_of(wrap(y - r // 8), wrap(z - (r // 2) % 4), (c + r % 2) % 2)

    def hail(r, carry):
        pl.semaphore_signal(bar, inc=1, device_id={"dev": other(r)}, device_id_type=MESH)
        return carry

    lax.fori_loop(1, 32, hail, 0)
    for r in range(1, 4):
        pl.semaphore_signal(bar, inc=1, device_id={"group": wrap(g + r)}, device_id_type=MESH)
    me = y * 4 + z
    loads = [
        pltpu.make_async_copy(x_hbm.at[pl.ds(b * 128, 128)], xall.at[me, c, b], local_sem.at[b])
        for b in range(2)
    ]
    loads.append(pltpu.make_async_copy(wg_hbm, wg, local_sem.at[2]))
    window = pl.multiple_of((d // 4) * 128, 128)
    for t in range(3):
        loads.append(
            pltpu.make_async_copy(
                wqkv_hbm.at[:, pl.ds(t * 1024 + window, 128)], w3.at[t], local_sem.at[3 + t]
            )
        )
    for src, dst in (
        (inner_hbm.at[0], inner_ref), (outer_hbm.at[0], outer_ref), (adj_hbm.at[0], adj.at[0, pl.ds(0, 16)]),
        (adj_hbm.at[1], adj.at[1, pl.ds(0, 16)]), (nb_hbm, nb), (blocks_hbm, blocks), (counts_hbm, counts),
        (wo_hbm, wo), (wu_hbm, wu), (wd_hbm, wd),
    ):
        loads.append(pltpu.make_async_copy(src, dst, local_sem.at[len(loads)]))
    for i in (0, 1, 6):
        loads[i].start()
    loads[6].wait()
    idx[me, c, :, 0:64] = inner_ref[...]
    idx[me, c, :, 64:128] = jnp.zeros((32, 64), jnp.int32)
    loads[0].wait()
    loads[1].wait()
    pl.semaphore_wait(bar, 34)
    started = []

    class Route:
        def __init__(self, b):
            self.b = b
            self.p, self.s = (y, z) if b == 0 else (z, y)

        def chip(self, dp, ds):
            p, s = wrap(self.p + dp), wrap(self.s + ds)
            return p * 4 + s if self.b == 0 else s * 4 + p

        def target(self, dp, ds):
            p, s = wrap(self.p + dp), wrap(self.s + ds)
            return dev_of(p, s, c) if self.b == 0 else dev_of(s, p, c)

        def view(self, dp, ds, half):
            r = xall.at[self.chip(dp, ds), c, self.b]
            return r if half is None else r.at[pl.ds(half * 64, 64)]

        def copies(self, tag, dp, ds, half, to):
            v = self.view(dp, ds, half)
            k = self.b * 20 + tag
            out = [
                pltpu.make_async_remote_copy(
                    v, v, send_sem.at[k], recv_sem.at[k], device_id={"dev": to}, device_id_type=MESH
                )
            ]
            if self.b == 0 and half != 1:
                v = idx.at[self.chip(dp, ds), c]
                out.append(
                    pltpu.make_async_remote_copy(
                        v, v, isend.at[tag], irecv.at[tag], device_id={"dev": to}, device_id_type=MESH
                    )
                )
            return out

        def send(self, tag, dp, ds, half, to_p, to_s):
            for copy in self.copies(tag, dp, ds, half, self.target(to_p, to_s)):
                copy.start()
                started.append(copy)

        def wait(self, tag, dp, ds, half=None):
            for copy in self.copies(tag, dp, ds, half, sib):
                copy.wait_recv()

        def sib_copy(self, dp, ds):
            i = self.chip(dp, ds)
            v = self.view(dp, ds, None)
            copies = [
                pltpu.make_async_remote_copy(
                    v, v, sib_send.at[i * 2 + self.b], sib_recv.at[i * 2 + self.b],
                    device_id={"dev": sib}, device_id_type=MESH,
                )
            ]
            if self.b == 0:
                v = idx.at[i, c]
                copies.append(
                    pltpu.make_async_remote_copy(
                        v, v, sibi_send.at[i], sibi_recv.at[i],
                        device_id={"dev": sib}, device_id_type=MESH,
                    )
                )
            for copy in copies:
                copy.start()
                started.append(copy)

    def sib_wait(chip):
        for b in range(2):
            v = xall.at[chip, 1 - c, b]
            pltpu.make_async_remote_copy(
                v, v, sib_send.at[chip * 2 + b], sib_recv.at[chip * 2 + b],
                device_id={"dev": sib}, device_id_type=MESH,
            ).wait_recv()
        v = idx.at[chip, 1 - c]
        pltpu.make_async_remote_copy(
            v, v, sibi_send.at[chip], sibi_recv.at[chip],
            device_id={"dev": sib}, device_id_type=MESH,
        ).wait_recv()

    lane = lax.broadcasted_iota(jnp.int32, (256, 128), 1)
    row = lax.broadcasted_iota(jnp.int32, (256, 64), 0)

    def add_block(t, block):
        for b in range(2):
            at = 16
            for s in range(16):
                at = jnp.where(nb[b, s] == t, s, at)
            acc[b] += dot(adj[b, at], block)

    def process(chip):
        sib_wait(chip)
        for cc in range(2):
            rows = xall[chip, cc].reshape(256, 1024)
            both = dot(rows, wc[...])
            at = chip * 4 + cc * 2
            q[pl.ds(at, 2)] = both[:, :128].astype(BF).reshape(2, 128, 128)
            kv[pl.ds(at, 2)] = (
                jnp.where(lane == ONES_LANE, 1.0, both[:, 128:]).astype(BF).reshape(2, 128, 128)
            )
            picks = idx[chip, cc, pl.ds(d, 1), :][:, 0:64]
            hot = jnp.where(row == picks, 1.0, 0.0).astype(BF)
            xsel[pl.ds(cc * 64, 64), :] = dot_tn(hot, rows).astype(BF)
        add_block(2 + chip, dot(xsel[...], wg[...]).astype(BF))

    def process_many(count, where):
        def step(i, carry):
            dy, dz = where(i)
            process(wrap(y + dy) * 4 + wrap(z + dz))
            return carry

        lax.fori_loop(0, count, step, 0)

    routes = [Route(0), Route(1)]
    for t in routes:
        t.send(0, 0, 0, None, 1, 0)
        t.send(1, 0, 0, None, -1, 0)
    for t in routes:
        t.send(4, 0, 0, None, 0, 1)
        t.send(5, 0, 0, None, 0, -1)
    for t in routes:
        t.sib_copy(0, 0)

    for i in (2, 3, 4, 5, 7, 8, 9, 10, 11, 12, 13, 14, 15):
        loads[i].start()

    loads[2].wait()
    own = dot(xall[me, c].reshape(256, 1024), wg[...]).astype(BF)
    loads[7].wait()
    for r in range(1, 4):
        to = wrap(g + r)
        hot = jnp.where(
            lax.broadcasted_iota(jnp.int32, (256, 128), 0) == outer_ref[pl.ds(to, 1), :], 1.0, 0.0
        ).astype(BF)
        outsel[r - 1] = dot_tn(hot, own).astype(BF)
        copy = pltpu.make_async_remote_copy(
            outsel.at[r - 1], outin.at[r - 1], out_send.at[r - 1], out_recv.at[r - 1],
            device_id={"group": to}, device_id_type=MESH,
        )
        copy.start()
        started.append(copy)

    for t in range(3):
        loads[3 + t].wait()
    take = lax.broadcasted_iota(jnp.int32, (128, 256), 0) - (d % 4) * HEAD
    col = lax.broadcasted_iota(jnp.int32, (128, 256), 1)
    total = jnp.zeros((1024, 256), F32)
    for t in range(3):
        first = (0, 128, 128 + HEAD)[t]
        inside = (take >= 0) & (take < HEAD) & (col == take + first)
        total = total + dot(w3[t], jnp.where(inside, 1.0, 0.0).astype(BF))
    wc[...] = total.astype(BF)

    def e1():
        for t in routes:
            t.wait(0, -1, 0)
            t.send(2, -1, 0, 0, 1, 0)
            t.wait(1, 1, 0)
            t.send(3, 1, 0, 1, -1, 0)
        for t in routes:
            for k in (1, 2):
                t.send(4 + 4 * k, STEPS[k], 0, None, 0, 1)
                t.send(5 + 4 * k, STEPS[k], 0, None, 0, -1)
                t.sib_copy(STEPS[k], 0)

    def e2():
        for t in routes:
            t.wait(2, 2, 0, 0)
            t.wait(3, 2, 0, 1)
            t.send(16, 2, 0, None, 0, 1)
            t.send(17, 2, 0, None, 0, -1)
            t.sib_copy(2, 0)

    def e3(k):
        for t in routes:
            t.wait(4 + 4 * k, STEPS[k], -1)
            t.send(6 + 4 * k, STEPS[k], -1, 0, 0, 1)
            t.wait(5 + 4 * k, STEPS[k], 1)
            t.send(7 + 4 * k, STEPS[k], 1, 1, 0, -1)
            t.sib_copy(STEPS[k], -1)
            t.sib_copy(STEPS[k], 1)

    def e4(k):
        for t in routes:
            t.wait(6 + 4 * k, STEPS[k], 2, 0)
            t.wait(7 + 4 * k, STEPS[k], 2, 1)
            t.sib_copy(STEPS[k], 2)

    def sign(i):
        return 1 - 2 * (i % 2)

    def own_blocks():
        for i in (8, 9, 10):
            loads[i].wait()
        for b in range(2):
            adj[b, 16] = jnp.zeros((128, 128), BF)
            acc[b] = jnp.zeros((128, 1024), F32)
        add_block(0, own[0:128])
        add_block(1, own[128:256])
        hot = jnp.where(
            lax.broadcasted_iota(jnp.int32, (256, 128), 0) == outer_ref[pl.ds(g, 1), :], 1.0, 0.0
        ).astype(BF)
        add_block(18 + g, dot_tn(hot, own).astype(BF))

    def outer_blocks():
        for r in range(1, 4):
            pltpu.make_async_remote_copy(
                outsel.at[r - 1], outin.at[r - 1], out_send.at[r - 1], out_recv.at[r - 1],
                device_id={"group": wrap(g + r)}, device_id_type=MESH,
            ).wait_recv()
            add_block(18 + wrap(g - r), outin[r - 1])

    own_blocks()
    e1()
    process_many(1, lambda i: (0 * i, 0 * i))
    e2()
    e3(0)
    process_many(2, lambda i: (sign(i), 0 * i))
    e3(1)
    process_many(2, lambda i: (0 * i, sign(i)))
    e3(2)
    outer_blocks()
    e3(3)
    process_many(4, lambda i: (sign(i), 1 - 2 * (i // 2)))
    e4(0)
    process_many(2, lambda i: (2 * i, 2 * (1 - i)))
    e4(1)
    process_many(2, lambda i: (3 * i - 1, 2 - 3 * i))
    e4(2)
    process_many(2, lambda i: (1 + i, 2 - i))
    e4(3)
    process_many(1, lambda i: (2 + 0 * i, 2 + 0 * i))
    kv[64] = jnp.zeros((128, 128), BF)

    factor = 1.4426950408889634 / HEAD**0.5
    slots = 16
    loads[11].wait()
    loads[12].wait()

    def score(i, scores, tops):
        query = q[i]
        highest = None
        for s in range(0, slots, 2):
            keys = [
                kv[jnp.where(s + u < counts[i], blocks[i, s + u], blocks[i, 0])] for u in range(2)
            ]
            part = dot_nt(query, jnp.concatenate(keys, axis=0))
            scores[:, pl.ds(s * 128, 256)] = part
            part = jnp.maximum(part[:, :128], part[:, 128:])
            highest = part if highest is None else jnp.maximum(highest, part)
        tops[...] = jnp.broadcast_to(jnp.max(highest, axis=1, keepdims=True) * factor, (128, 128))

    def mix(i, to, lanes, scores, tops):
        top = jnp.concatenate([tops[...]] * 2, axis=1)
        mixed = None
        for s in range(0, slots, 2):
            probs = jnp.exp2(scores[:, pl.ds(s * 128, 256)] * factor - top).astype(BF)
            values = [kv[jnp.where(s + u < counts[i], blocks[i, s + u], 64)] for u in range(2)]
            part = dot(probs, jnp.concatenate(values, axis=0))
            mixed = part if mixed is None else mixed + part
        turned = mixed.T
        part = turned[HEAD : 2 * HEAD] / turned[ONES_LANE : ONES_LANE + 1]
        ob[to, :, lanes * 128 : lanes * 128 + 128] = part.astype(BF)

    def give(r):
        return pltpu.make_async_remote_copy(
            ob.at[other(r)], ret.at[d], ret_send.at[r], ret_recv.at[r],
            device_id={"dev": other(r)}, device_id_type=MESH,
        )

    def take_in(r):
        return pltpu.make_async_remote_copy(
            ob.at[other(r)], ret.at[source(r)], ret_send.at[r], ret_recv.at[r],
            device_id={"dev": other(r)}, device_id_type=MESH,
        )

    score(other(31) * 2, s_a, m_a)

    def attend(n, carry):
        r = 31 - n
        to = other(r)
        score(to * 2 + 1, s_b, m_b)
        mix(to * 2, to, 0, s_a, m_a)
        score(other((r + 31) % 32) * 2, s_a, m_a)
        mix(to * 2 + 1, to, 1, s_b, m_b)

        @pl.when(r > 0)
        def _():
            give(r).start()

        return carry

    lax.fori_loop(0, 32, attend, 0)
    ret[d] = ob[d]
    features = xall[me, c].reshape(256, 1024).astype(F32)
    local = layer_norm(features + acc[...].reshape(256, 1024))
    loads[13].wait()

    def land(r, carry):
        take_in(r).wait_recv()
        return carry

    lax.fori_loop(1, 32, land, 0)
    projected = dot_tn(ret[...].reshape(1024, 256), wo[...])
    summed = local + layer_norm(features + projected)
    acc[...] = summed.reshape(2, 128, 1024)
    loads[14].wait()
    hidden = jax.nn.gelu(dot(summed.astype(BF), wu[...])).astype(BF)
    loads[15].wait()
    o_ref[...] = layer_norm(acc[...].reshape(256, 1024) + dot(hidden, wd[...])).astype(BF)

    for copy in started:
        copy.wait_send()

    def leave(r, carry):
        give(r).wait_send()
        return carry

    lax.fori_loop(1, 32, leave, 0)


def per_device(
    node_feats, w_gcn, adj_tiles, neighbor_blocks, inner_rows, outer_rows,
    w_qkv, key_blocks, key_counts, w_out, w_up, w_down,
):
    hbm = pl.BlockSpec(memory_space=pl.ANY)
    dma = pltpu.SemaphoreType.DMA
    return pl.pallas_call(
        layer_kernel,
        out_shape=jax.ShapeDtypeStruct((256, 1024), BF),
        in_specs=[hbm] * 12,
        out_specs=pl.BlockSpec(memory_space=pltpu.VMEM),
        scratch_shapes=[
            pltpu.VMEM((16, 2, 2, 128, 1024), BF),
            pltpu.VMEM((16, 2, 32, 128), jnp.int32),
            pltpu.VMEM((1024, 1024), BF),
            pltpu.VMEM((3, 1024, 128), BF),
            pltpu.VMEM((1024, 256), BF),
            pltpu.VMEM((128, 1024), BF),
            pltpu.VMEM((64, 128, 128), BF),
            pltpu.VMEM((65, 128, 128), BF),
            pltpu.VMEM((3, 128, 1024), BF),
            pltpu.VMEM((3, 128, 1024), BF),
            pltpu.VMEM((32, 64), jnp.int32),
            pltpu.VMEM((4, 128), jnp.int32),
            pltpu.VMEM((2, 17, 128, 128), BF),
            pltpu.VMEM((2, 128, 1024), F32),
            pltpu.VMEM((1024, 1024), BF),
            pltpu.VMEM((1024, 2048), BF),
            pltpu.VMEM((2048, 1024), BF),
            pltpu.VMEM((32, 32, 256), BF),
            pltpu.VMEM((32, 32, 256), BF),
            pltpu.VMEM((128, 2048), F32),
            pltpu.VMEM((128, 2048), F32),
            pltpu.VMEM((128, 128), F32),
            pltpu.VMEM((128, 128), F32),
            pltpu.SMEM((2, 16), jnp.int32),
            pltpu.SMEM((64, 16), jnp.int32),
            pltpu.SMEM((64,), jnp.int32),
            dma((40,)), dma((40,)), dma((20,)), dma((20,)), dma((32,)), dma((32,)), dma((16,)), dma((16,)),
            dma((3,)), dma((3,)), dma((16,)), dma((32,)), dma((32,)),
        ],
        compiler_params=pltpu.CompilerParams(
            collective_id=0, has_side_effects=True, vmem_limit_bytes=56 << 20
        ),
        name="layer",
    )(
        node_feats, w_gcn, w_qkv, inner_rows, outer_rows, adj_tiles, neighbor_blocks,
        key_blocks, key_counts, w_out, w_up, w_down,
    )


def solution(mesh):
    placed = (
        P(("group", "dev"), None),
        P(),
        P(("group", "dev"), None, None, None),
        P(("group", "dev"), None),
        P(("group", "dev"), None, None),
        P(("group", "dev"), None, None),
        P(),
        P("group", None),
        P("group"),
        P(),
        P(),
        P(),
    )
    return jax.shard_map(
        per_device, mesh=mesh, in_specs=placed, out_specs=P(("group", "dev"), None), check_vma=False
    )
```

time: 124 us -> 102 us (0.82)
  Pallas kernels: 117 us -> 98.3 us
  local copies, waits for them, and re-layouts: 6.62 us -> 3.26 us
    pallas_call x3 -> x1, Pallas kernels: 117 us -> 98.3 us  [per_device(): pl.pallas_call(layer_kernel, out_shape=jax.ShapeDtypeStruct((256, 1024),...]
    unnamed x10 -> x2, local copies, waits for them, and re-layouts: 6.62 us -> 3.26 us
where the time goes in v3:
time: 102 us
  Pallas kernels  98.3 us (96%)
  local copies, waits for them, and re-layouts  3.26 us (3%)
    pallas_call x1, Pallas kernels, per_device(): pl.pallas_call(layer_kernel, out_shape=jax.ShapeDtypeStruct((256, 1024),...  98.3 us
    unnamed x2, local copies, waits for them, and re-layouts  3.26 us

profile of v3, /device:TPU:1, one launch (start us, length us, event | category | flops | bytes accessed | tf_op | source)
XLA Modules:
  0.0 101.5 jit_solution(11114550041883754901)
XLA Ops:
  0.0 1.4 %copy.13.blocks_hbm = s32[64,16]{1,0:T(8,128)} copy(s32[64,16]{0,1:T(8,128)} %param.19) | data formatting | bytes 8192 | tf_op args[7]
  1.4 98.3 %layer.1 = bf16[256,1024]{1,0:T(8,128)(2,1)} custom-call(bf16[256,1024]{1,0:T(8,128)(2,1)} %x_hbm.1, bf16[1024,1024]{1,0:T(8,128)(2,1)} %wg_hbm.1, bf16[1024,3072]{1,0:T(8,128)(2,1)} %wqkv_hbm.1, s32[1,32,64]{2,1,0:T(8,128)} %inner_hbm.1, s32[1,4,128]{2,1,0:T(4,128)} %outer_hbm.1, bf16[2,16,128,128]{3,2,1,0:T(8,128)(2,1)} %adj_hbm.1, s32[2,16]{1,0:T(2,128)} %nb_hbm.1, ...), custom_call_target="tpu_custom_call" | custom-call | tf_op jit(solution)/shard_map/layer/pallas_call | solution.py:430
  99.7 1.9 %copy.15 = bf16[256,1024]{1,0:T(8,128)(2,1)} copy(bf16[256,1024]{1,0:T(8,128)(2,1)} %layer.1) | data formatting | bytes 1048576

commit v4 on v3

v4 whole, which is shorter than its diff:
```python
import jax
import jax.numpy as jnp
from jax import lax
from jax.experimental import pallas as pl
from jax.experimental.pallas import tpu as pltpu
from jax.sharding import PartitionSpec as P

MESH = pl.DeviceIdType.MESH
BF = jnp.bfloat16
F32 = jnp.float32
HEADS = 32
HEAD = 32
RING = 4
HALF = 512


def wrap(v):
    return (v + RING) % RING


def place():
    d = lax.axis_index("dev")
    return d, d // 8, (d // 2) % 4, d % 2


def dev_of(y, z, c):
    return y * 8 + z * 2 + c


def dot(a, b):
    return jnp.dot(a, b, preferred_element_type=F32)


def dot_nt(a, b):
    return lax.dot_general(a, b, (((1,), (1,)), ((), ())), preferred_element_type=F32)


def dot_tn(a, b):
    return lax.dot_general(a, b, (((0,), (0,)), ((), ())), preferred_element_type=F32)


def layer_norm(values):
    average = jnp.mean(values, axis=-1, keepdims=True)
    centered = values - average
    variance = jnp.mean(centered * centered, axis=-1, keepdims=True)
    return centered / jnp.sqrt(variance + 1e-05)


def layer_kernel(
    x_hbm, wg_hbm, wqkv_hbm, inner_hbm, outer_hbm, adj_hbm, nb_hbm, blocks_hbm, counts_hbm,
    wo_hbm, wu_hbm, wd_hbm,
    o_ref,
    x, wg, w, heads, qkv, query, value, own, ring, idx, picked, inner, outsel, outin, inner_ref, outer_ref, adj, acc,
    wo, wu, wd, ob, ret, s_a, s_b, m_a, m_b, nb, blocks, counts,
    qkv_send, qkv_recv, ring_send, ring_recv, idx_send, idx_recv, pick_send, pick_recv,
    out_send, out_recv, local_sem, w_sem, ret_send, ret_recv,
):
    d, y, z, c = place()
    g = lax.axis_index("group")
    bar = pltpu.get_barrier_semaphore()

    def other(r):
        return dev_of(wrap(y + r // 8), wrap(z + (r // 2) % 4), (c + r % 2) % 2)

    def source(r):
        return dev_of(wrap(y - r // 8), wrap(z - (r // 2) % 4), (c + r % 2) % 2)

    def hail(r, carry):
        pl.semaphore_signal(bar, inc=1, device_id={"dev": other(r)}, device_id_type=MESH)
        return carry

    lax.fori_loop(1, 32, hail, 0)
    for r in range(1, 4):
        pl.semaphore_signal(bar, inc=1, device_id={"group": wrap(g + r)}, device_id_type=MESH)

    pairs = (
        (x_hbm, x), (wg_hbm, wg), (inner_hbm.at[0], inner_ref), (outer_hbm.at[0], outer_ref),
        (adj_hbm.at[0], adj.at[0, pl.ds(0, 16)]), (adj_hbm.at[1], adj.at[1, pl.ds(0, 16)]),
        (nb_hbm, nb), (blocks_hbm, blocks), (counts_hbm, counts),
        (wo_hbm, wo), (wu_hbm, wu), (wd_hbm, wd),
    )
    loads = [
        pltpu.make_async_copy(src, dst, local_sem.at[i]) for i, (src, dst) in enumerate(pairs)
    ]

    def window(n):
        return (d // 4 + 3 * n) % 8

    def w_load(n, t):
        at = pl.multiple_of(t * 1024 + window(n) * 128, 128)
        return pltpu.make_async_copy(
            wqkv_hbm.at[:, pl.ds(at, 128)], w.at[n, :, pl.ds(t * 128, 128)], w_sem.at[n * 3 + t]
        )

    for load in loads[:4]:
        load.start()
    for n in range(8):
        for t in range(3):
            w_load(n, t).start()
    for load in loads[4:9]:
        load.start()
    tail = jnp.where(lax.broadcasted_iota(jnp.int32, (16, 128), 0) == 0, 1.0, 0.0).astype(BF)
    for i in range(64):
        qkv[i, 96:112, :] = tail
    loads[0].wait()
    pl.semaphore_wait(bar, 34)

    def qkv_copy(to):
        return pltpu.make_async_remote_copy(
            heads.at[to], qkv.at[pl.ds(2 * d, 2), pl.ds(0, 96)], qkv_send.at[to], qkv_recv.at[d],
            device_id={"dev": to}, device_id_type=MESH,
        )

    def qkv_land(src):
        return pltpu.make_async_remote_copy(
            heads.at[src], qkv.at[pl.ds(2 * src, 2), pl.ds(0, 96)], qkv_send.at[src], qkv_recv.at[src],
            device_id={"dev": src}, device_id_type=MESH,
        )

    def project(n, carry):
        for t in range(3):
            w_load(n, t).wait()
        turned = dot(x[...], w[n]).T.astype(BF)
        for k in range(4):
            to = window(n) * 4 + k
            for t in range(3):
                rows = turned[t * 128 + k * 32 : t * 128 + k * 32 + 32]
                for b in range(2):
                    heads[to, b, t * 32 : t * 32 + 32, :] = rows[:, b * 128 : b * 128 + 128]

            @pl.when(to != d)
            def _():
                qkv_copy(to).start()

        return carry

    loads[1].wait()
    own[...] = dot(x[...], wg[...]).astype(BF)
    loads[2].wait()
    lists = [inner_ref[pl.ds(k, 16, 2), :] for k in range(2)]

    class Route:
        def __init__(self, h):
            self.h = h
            self.p, self.s = (z, y) if h == 0 else (y, z)

        def chip(self, p, s):
            return s * 4 + p if self.h == 0 else p * 4 + s

        def target(self, dp, ds, cc):
            return self.chip(wrap(self.p + dp), wrap(self.s + ds)) * 2 + cc

        def copies(self, tag, dp, half, to):
            v = ring.at[self.h, wrap(self.p + dp)]
            if half is not None:
                v = v.at[pl.ds(half * 128, 128)]
            k = self.h * 4 + tag
            out = [
                pltpu.make_async_remote_copy(
                    v, v, ring_send.at[k], ring_recv.at[k], device_id={"dev": to}, device_id_type=MESH
                )
            ]
            if tag < 3:
                v = idx.at[self.h, wrap(self.p + dp)]
                out.append(
                    pltpu.make_async_remote_copy(
                        v, v, idx_send.at[k], idx_recv.at[k], device_id={"dev": to}, device_id_type=MESH
                    )
                )
            return out

        def send(self, tag, dp, half, to_p):
            for copy in self.copies(tag, dp, half, self.target(to_p, 0, c)):
                copy.start()
                started.append(copy)

        def wait(self, tag, dp, half=None):
            for copy in self.copies(tag, dp, half, self.target(1, 0, c)):
                copy.wait_recv()

        def pick(self, dp, ds):
            p = wrap(self.p + dp)
            row = self.chip(self.p, wrap(self.s + ds))
            hot = jnp.where(
                lax.broadcasted_iota(jnp.int32, (256, 128), 0) == idx[self.h, p, pl.ds(row, 1), :],
                1.0, 0.0,
            ).astype(BF)
            rows = dot_tn(hot, ring[self.h, p]).astype(BF)
            for cc in range(2):
                picked[self.h, ds, cc, p] = rows[cc * 64 : cc * 64 + 64]

        def pick_copy(self, ds, dc):
            cc = (c + dc) % 2
            k = self.h * 8 + ds * 2 + dc
            return pltpu.make_async_remote_copy(
                picked.at[self.h, ds, cc], inner.at[self.h, self.s, c], pick_send.at[k], pick_recv.at[k],
                device_id={"dev": self.target(0, ds, cc)}, device_id_type=MESH,
            )

        def pick_land(self, ds, dc):
            cc = (c + dc) % 2
            k = self.h * 8 + ds * 2 + dc
            return pltpu.make_async_remote_copy(
                picked.at[self.h, ds, cc], inner.at[self.h, wrap(self.s - ds), cc],
                pick_send.at[k], pick_recv.at[k],
                device_id={"dev": self.target(0, ds, cc)}, device_id_type=MESH,
            )

    started = []
    routes = [Route(0), Route(1)]
    for t in routes:
        ring[t.h, t.p] = own[:, t.h * HALF : t.h * HALF + HALF]
        idx[t.h, t.p, :, 0:64] = lists[0]
        idx[t.h, t.p, :, 64:128] = lists[1]
    for t in routes:
        t.send(0, 0, None, 1)
        t.send(1, 0, None, -1)

    lax.fori_loop(0, 8, project, 0)
    for load in loads[9:]:
        load.start()

    def outer_rows(to):
        hot = jnp.where(
            lax.broadcasted_iota(jnp.int32, (256, 128), 0) == outer_ref[pl.ds(to, 1), :], 1.0, 0.0
        ).astype(BF)
        return dot_tn(hot, own[...]).astype(BF)

    def outer_copy(r):
        return pltpu.make_async_remote_copy(
            outsel.at[r - 1], outin.at[r - 1], out_send.at[r - 1], out_recv.at[r - 1],
            device_id={"group": wrap(g + r)}, device_id_type=MESH,
        )

    loads[3].wait()
    for r in range(1, 4):
        outsel[r - 1] = outer_rows(wrap(g + r))
        outer_copy(r).start()
        started.append(outer_copy(r))

    def picks(t, count, where):
        def step(i, carry):
            t.pick(*where(i))
            return carry

        lax.fori_loop(0, count, step, 0)

    for t in routes:
        picks(t, 4, lambda i: (0 * i, i))

    def add_block(t, block):
        for b in range(2):
            at = 16
            for s in range(16):
                at = jnp.where(nb[b, s] == t, s, at)
            acc[b] += dot(adj[b, at], block)

    for i in (4, 5, 6):
        loads[i].wait()
    for b in range(2):
        adj[b, 16] = jnp.zeros((128, 128), BF)
        acc[b] = jnp.zeros((128, 1024), F32)
    add_block(0, own[0:128, :])
    add_block(1, own[128:256, :])
    add_block(18 + g, outer_rows(g))

    for t in routes:
        t.wait(0, -1)
        t.send(2, -1, 0, 1)
        t.wait(1, 1)
        t.send(3, 1, 1, -1)
    for t in routes:
        picks(t, 8, lambda i: (1 - 2 * (i // 4), i % 4))
    for t in routes:
        t.wait(2, 2, 0)
        t.wait(3, 2, 1)
        picks(t, 4, lambda i: (2 + 0 * i, i))
    for t in routes:
        inner[t.h, t.s, c] = picked[t.h, 0, c]
    for r in range(1, 4):
        outer_copy(r).wait_recv()
        add_block(18 + wrap(g - r), outin[r - 1])

    qkv[pl.ds(2 * d, 2), pl.ds(0, 96)] = heads[d]

    def turn(src):
        for b in range(2):
            i = 2 * src + b
            query[i] = qkv[i, 0:32, :].astype(F32).T.astype(BF)
            value[i] = qkv[i, 64:112, :].astype(F32).T.astype(BF)

    turn(d)
    value[64] = jnp.zeros((128, 48), BF)

    def arrive(n, carry):
        src = source((5 * n) % 32)
        qkv_land(src).wait_recv()
        turn(src)
        return carry

    lax.fori_loop(1, 32, arrive, 0)
    hops = [(2, 0), (2, 1), (1, 0), (1, 1), (3, 0), (3, 1), (0, 1)]
    for ds, dc in hops:
        for t in routes:
            t.pick_copy(ds, dc).start()

    factor = 1.4426950408889634 / HEAD**0.5
    slots = 16
    loads[7].wait()
    loads[8].wait()

    def score(i, scores, tops):
        highest = None
        for s in range(0, slots, 2):
            keys = [
                qkv[jnp.where(s + u < counts[i], blocks[s + u, i], blocks[0, i]), 32:64, :]
                for u in range(2)
            ]
            part = dot(query[i], jnp.concatenate(keys, axis=1))
            scores[:, pl.ds(s * 128, 256)] = part
            part = jnp.maximum(part[:, :128], part[:, 128:])
            highest = part if highest is None else jnp.maximum(highest, part)
        tops[...] = jnp.broadcast_to(jnp.max(highest, axis=1, keepdims=True) * factor, (128, 128))

    def mix(i, to, lanes, scores, tops):
        top = jnp.concatenate([tops[...]] * 2, axis=1)
        mixed = None
        for s in range(0, slots, 2):
            probs = jnp.exp2(scores[:, pl.ds(s * 128, 256)] * factor - top).astype(BF)
            values = [
                value[jnp.where(s + u < counts[i], blocks[s + u, i], 64)] for u in range(2)
            ]
            part = dot(probs, jnp.concatenate(values, axis=0))
            mixed = part if mixed is None else mixed + part
        mixed = mixed.T
        part = mixed[0:32] / mixed[32:33]
        ob[to, :, lanes * 128 : lanes * 128 + 128] = part.astype(BF)

    def give(r):
        return pltpu.make_async_remote_copy(
            ob.at[other(r)], ret.at[d], ret_send.at[r], ret_recv.at[r],
            device_id={"dev": other(r)}, device_id_type=MESH,
        )

    def take_in(r):
        return pltpu.make_async_remote_copy(
            ob.at[other(r)], ret.at[source(r)], ret_send.at[r], ret_recv.at[r],
            device_id={"dev": other(r)}, device_id_type=MESH,
        )

    score(other(31) * 2, s_a, m_a)

    def attend(n, carry):
        r = 31 - n
        to = other(r)
        score(to * 2 + 1, s_b, m_b)
        mix(to * 2, to, 0, s_a, m_a)
        score(other((r + 31) % 32) * 2, s_a, m_a)
        mix(to * 2 + 1, to, 1, s_b, m_b)

        @pl.when(r > 0)
        def _():
            give(r).start()

        return carry

    lax.fori_loop(0, 32, attend, 0)
    ret[d] = ob[d]

    for ds, dc in reversed(hops):
        for t in routes:
            t.pick_land(ds, dc).wait_recv()

    def gathered(row, carry):
        parts = []
        for col in range(4):
            left = inner[0, row, :, col].reshape(128, HALF)
            right = inner[1, col, :, row].reshape(128, HALF)
            parts.append(jnp.concatenate([left, right], axis=1))
        table = jnp.concatenate(parts, axis=0)
        for b in range(2):
            tiles = []
            for col in range(4):
                at = 16
                for s in range(16):
                    at = jnp.where(nb[b, s] == 2 + row * 4 + col, s, at)
                tiles.append(adj[b, at])
            acc[b] += dot(jnp.concatenate(tiles, axis=1), table)
        return carry

    lax.fori_loop(0, 4, gathered, 0)
    features = x[...].astype(F32)
    local = layer_norm(features + acc[...].reshape(256, 1024))
    loads[9].wait()

    def land(r, carry):
        take_in(r).wait_recv()
        return carry

    lax.fori_loop(1, 32, land, 0)
    projected = dot_tn(ret[...].reshape(1024, 256), wo[...])
    summed = local + layer_norm(features + projected)
    acc[...] = summed.reshape(2, 128, 1024)
    loads[10].wait()
    hidden = jax.nn.gelu(dot(summed.astype(BF), wu[...])).astype(BF)
    loads[11].wait()
    o_ref[...] = layer_norm(acc[...].reshape(256, 1024) + dot(hidden, wd[...])).astype(BF)

    for copy in started:
        copy.wait_send()
    for ds, dc in hops:
        for t in routes:
            t.pick_copy(ds, dc).wait_send()

    def leave(r, carry):
        give(r).wait_send()
        qkv_copy((d + r) % 32).wait_send()
        return carry

    lax.fori_loop(1, 32, leave, 0)


def per_device(
    node_feats, w_gcn, adj_tiles, neighbor_blocks, inner_rows, outer_rows,
    w_qkv, key_blocks, key_counts, w_out, w_up, w_down,
):
    hbm = pl.BlockSpec(memory_space=pl.ANY)
    dma = pltpu.SemaphoreType.DMA
    return pl.pallas_call(
        layer_kernel,
        out_shape=jax.ShapeDtypeStruct((256, 1024), BF),
        in_specs=[hbm] * 12,
        out_specs=pl.BlockSpec(memory_space=pltpu.VMEM),
        scratch_shapes=[
            pltpu.VMEM((256, 1024), BF),
            pltpu.VMEM((1024, 1024), BF),
            pltpu.VMEM((8, 1024, 384), BF),
            pltpu.VMEM((32, 2, 96, 128), BF),
            pltpu.VMEM((64, 112, 128), BF),
            pltpu.VMEM((64, 128, 32), BF),
            pltpu.VMEM((65, 128, 48), BF),
            pltpu.VMEM((256, 1024), BF),
            pltpu.VMEM((2, 4, 256, HALF), BF),
            pltpu.VMEM((2, 4, 16, 128), jnp.int32),
            pltpu.VMEM((2, 4, 2, 4, 64, HALF), BF),
            pltpu.VMEM((2, 4, 2, 4, 64, HALF), BF),
            pltpu.VMEM((3, 128, 1024), BF),
            pltpu.VMEM((3, 128, 1024), BF),
            pltpu.VMEM((32, 64), jnp.int32),
            pltpu.VMEM((4, 128), jnp.int32),
            pltpu.VMEM((2, 17, 128, 128), BF),
            pltpu.VMEM((2, 128, 1024), F32),
            pltpu.VMEM((1024, 1024), BF),
            pltpu.VMEM((1024, 2048), BF),
            pltpu.VMEM((2048, 1024), BF),
            pltpu.VMEM((32, 32, 256), BF),
            pltpu.VMEM((32, 32, 256), BF),
            pltpu.VMEM((128, 2048), F32),
            pltpu.VMEM((128, 2048), F32),
            pltpu.VMEM((128, 128), F32),
            pltpu.VMEM((128, 128), F32),
            pltpu.SMEM((2, 16), jnp.int32),
            pltpu.SMEM((16, 64), jnp.int32),
            pltpu.SMEM((64,), jnp.int32),
            dma((32,)), dma((32,)), dma((8,)), dma((8,)), dma((8,)), dma((8,)), dma((16,)), dma((16,)),
            dma((3,)), dma((3,)), dma((12,)), dma((24,)), dma((32,)), dma((32,)),
        ],
        compiler_params=pltpu.CompilerParams(
            collective_id=0, has_side_effects=True, vmem_limit_bytes=58 << 20
        ),
        name="layer",
    )(
        node_feats, w_gcn, w_qkv, inner_rows, outer_rows, adj_tiles, neighbor_blocks,
        key_blocks.T, key_counts, w_out, w_up, w_down,
    )


def solution(mesh):
    placed = (
        P(("group", "dev"), None),
        P(),
        P(("group", "dev"), None, None, None),
        P(("group", "dev"), None),
        P(("group", "dev"), None, None),
        P(("group", "dev"), None, None),
        P(),
        P("group", None),
        P("group"),
        P(),
        P(),
        P(),
    )
    return jax.shard_map(
        per_device, mesh=mesh, in_specs=placed, out_specs=P(("group", "dev"), None), check_vma=False
    )
```

time: 102 us -> 85.3 us (0.84)
  Pallas kernels: 98.3 us -> 83.3 us
  local copies, waits for them, and re-layouts: 3.26 us -> 1.87 us
    pallas_call x1, Pallas kernels: 98.3 us -> 83.3 us  [per_device(): pl.pallas_call(layer_kernel, out_shape=jax.ShapeDtypeStruct((256, 1024),...]
    unnamed x2 -> x1, local copies, waits for them, and re-layouts: 3.26 us -> 1.87 us
where the time goes in v4:
time: 85.3 us; the launch traced here: 85.2 us
  Pallas kernels  83.3 us (98%)
  local copies, waits for them, and re-layouts  1.87 us (2%)
    pallas_call x1, Pallas kernels, per_device(): pl.pallas_call(layer_kernel, out_shape=jax.ShapeDtypeStruct((256, 1024),...  83.3 us
    unnamed x1, local copies, waits for them, and re-layouts  1.87 us

profile of v4, /device:TPU:1, one launch (start us, length us, event | category | flops | bytes accessed | tf_op | source)
XLA Modules:
  0.0 85.2 jit_solution(8216376258060802082)
XLA Ops:
  0.0 83.3 %layer.1 = bf16[256,1024]{1,0:T(8,128)(2,1)} custom-call(bf16[256,1024]{1,0:T(8,128)(2,1)} %x_hbm.1, bf16[1024,1024]{1,0:T(8,128)(2,1)} %wg_hbm.1, bf16[1024,3072]{1,0:T(8,128)(2,1)} %wqkv_hbm.1, s32[1,32,64]{2,1,0:T(8,128)} %inner_hbm.1, s32[1,4,128]{2,1,0:T(4,128)} %outer_hbm.1, bf16[2,16,128,128]{3,2,1,0:T(8,128)(2,1)} %adj_hbm.1, s32[2,16]{1,0:T(2,128)} %nb_hbm.1, ...), custom_call_target="tpu_custom_call" | custom-call | tf_op jit(solution)/shard_map/layer/pallas_call | solution.py:429
  83.3 1.9 %copy.14 = bf16[256,1024]{1,0:T(8,128)(2,1)} copy(bf16[256,1024]{1,0:T(8,128)(2,1)} %layer.1) | data formatting | bytes 1048576

commit v5 on v4

--- a/solution.py
+++ b/solution.py
@@ -84,7 +84,7 @@
     ]
 
     def window(n):
-        return (d // 4 + 3 * n) % 8
+        return (d // 4 + 5 * n) % 8
 
     def w_load(n, t):
         at = pl.multiple_of(t * 1024 + window(n) * 128, 128)
@@ -103,7 +103,6 @@
     for i in range(64):
         qkv[i, 96:112, :] = tail
     loads[0].wait()
-    pl.semaphore_wait(bar, 34)
 
     def qkv_copy(to):
         return pltpu.make_async_remote_copy(
@@ -212,6 +211,7 @@
         ring[t.h, t.p] = own[:, t.h * HALF : t.h * HALF + HALF]
         idx[t.h, t.p, :, 0:64] = lists[0]
         idx[t.h, t.p, :, 64:128] = lists[1]
+    pl.semaphore_wait(bar, 34)
     for t in routes:
         t.send(0, 0, None, 1)
         t.send(1, 0, None, -1)
@@ -281,6 +281,11 @@
         outer_copy(r).wait_recv()
         add_block(18 + wrap(g - r), outin[r - 1])
 
+    hops = [(2, 0), (2, 1), (1, 0), (1, 1), (3, 0), (3, 1), (0, 1)]
+    for ds, dc in hops:
+        for t in routes:
+            t.pick_copy(ds, dc).start()
+
     qkv[pl.ds(2 * d, 2), pl.ds(0, 96)] = heads[d]
 
     def turn(src):
@@ -299,11 +304,6 @@
         return carry
 
     lax.fori_loop(1, 32, arrive, 0)
-    hops = [(2, 0), (2, 1), (1, 0), (1, 1), (3, 0), (3, 1), (0, 1)]
-    for ds, dc in hops:
-        for t in routes:
-            t.pick_copy(ds, dc).start()
-
     factor = 1.4426950408889634 / HEAD**0.5
     slots = 16
     loads[7].wait()

time: 85.3 us -> 81.4 us (0.954)
  Pallas kernels: 83.3 us -> 79.3 us
    pallas_call x1, Pallas kernels: 83.3 us -> 79.3 us  [per_device(): pl.pallas_call(layer_kernel, out_shape=jax.ShapeDtypeStruct((256, 1024),...]
where the time goes in v5:
time: 81.4 us; the launch traced here: 81.2 us
  Pallas kernels  79.3 us (97%)
  local copies, waits for them, and re-layouts  1.87 us (2%)
    pallas_call x1, Pallas kernels, per_device(): pl.pallas_call(layer_kernel, out_shape=jax.ShapeDtypeStruct((256, 1024),...  79.3 us
    unnamed x1, local copies, waits for them, and re-layouts  1.87 us

profile of v5, /device:TPU:1, one launch (start us, length us, event | category | flops | bytes accessed | tf_op | source)
XLA Modules:
  0.0 81.2 jit_solution(6219973245907627427)
XLA Ops:
  0.0 79.3 %layer.1 = bf16[256,1024]{1,0:T(8,128)(2,1)} custom-call(bf16[256,1024]{1,0:T(8,128)(2,1)} %x_hbm.1, bf16[1024,1024]{1,0:T(8,128)(2,1)} %wg_hbm.1, bf16[1024,3072]{1,0:T(8,128)(2,1)} %wqkv_hbm.1, s32[1,32,64]{2,1,0:T(8,128)} %inner_hbm.1, s32[1,4,128]{2,1,0:T(4,128)} %outer_hbm.1, bf16[2,16,128,128]{3,2,1,0:T(8,128)(2,1)} %adj_hbm.1, s32[2,16]{1,0:T(2,128)} %nb_hbm.1, ...), custom_call_target="tpu_custom_call" | custom-call | tf_op jit(solution)/shard_map/layer/pallas_call | solution.py:429
  79.3 1.9 %copy.14 = bf16[256,1024]{1,0:T(8,128)(2,1)} copy(bf16[256,1024]{1,0:T(8,128)(2,1)} %layer.1) | data formatting | bytes 1048576

commit v6 on v5

--- a/solution.py
+++ b/solution.py
@@ -84,7 +84,7 @@
     ]
 
     def window(n):
-        return (d // 4 + 5 * n) % 8
+        return (d // 4 + 5 * n + 4) % 8
 
     def w_load(n, t):
         at = pl.multiple_of(t * 1024 + window(n) * 128, 128)
@@ -93,11 +93,6 @@
         )
 
     for load in loads[:4]:
-        load.start()
-    for n in range(8):
-        for t in range(3):
-            w_load(n, t).start()
-    for load in loads[4:9]:
         load.start()
     tail = jnp.where(lax.broadcasted_iota(jnp.int32, (16, 128), 0) == 0, 1.0, 0.0).astype(BF)
     for i in range(64):
@@ -134,6 +129,11 @@
         return carry
 
     loads[1].wait()
+    for n in range(8):
+        for t in range(3):
+            w_load(n, t).start()
+    for load in loads[4:9]:
+        load.start()
     own[...] = dot(x[...], wg[...]).astype(BF)
     loads[2].wait()
     lists = [inner_ref[pl.ds(k, 16, 2), :] for k in range(2)]

time: 81.4 us -> 81.2 us (level)
  no operation moved by 1% of the time
where the time goes in v6:
time: 81.2 us; the launch traced here: 80.9 us
  Pallas kernels  79 us (97%)
  local copies, waits for them, and re-layouts  1.87 us (2%)
    pallas_call x1, Pallas kernels, per_device(): pl.pallas_call(layer_kernel, out_shape=jax.ShapeDtypeStruct((256, 1024),...  79 us
    unnamed x1, local copies, waits for them, and re-layouts  1.87 us

profile of v6, /device:TPU:1, one launch (start us, length us, event | category | flops | bytes accessed | tf_op | source)
XLA Modules:
  0.0 80.9 jit_solution(10788312196063930155)
XLA Ops:
  0.0 79.0 %layer.1 = bf16[256,1024]{1,0:T(8,128)(2,1)} custom-call(bf16[256,1024]{1,0:T(8,128)(2,1)} %x_hbm.1, bf16[1024,1024]{1,0:T(8,128)(2,1)} %wg_hbm.1, bf16[1024,3072]{1,0:T(8,128)(2,1)} %wqkv_hbm.1, s32[1,32,64]{2,1,0:T(8,128)} %inner_hbm.1, s32[1,4,128]{2,1,0:T(4,128)} %outer_hbm.1, bf16[2,16,128,128]{3,2,1,0:T(8,128)(2,1)} %adj_hbm.1, s32[2,16]{1,0:T(2,128)} %nb_hbm.1, ...), custom_call_target="tpu_custom_call" | custom-call | tf_op jit(solution)/shard_map/layer/pallas_call | solution.py:429
  79.0 1.9 %copy.14 = bf16[256,1024]{1,0:T(8,128)(2,1)} copy(bf16[256,1024]{1,0:T(8,128)(2,1)} %layer.1) | data formatting | bytes 1048576
